TPU v7x, 32 devices: a whole 2x2x4 slice. The times are simulated.
32 devices in a mesh: blk: 8 (over y, x, core), batch: 4 (over z).
Axes of the slice: x: 2, y: 2, z: 4, core: 2. Of those that a mesh axis runs over, the one named last changes fastest.
Arguments:
- query_base: bfloat16 [32, 36864], P(('batch', 'blk')), may hold values from -14 to 14
- query_latent: bfloat16 [32, 1536], P(('batch', 'blk')), may hold values from -6 to 6
- tenant_ids: int32 [32], P('batch'), may hold values from 0 to 3
- adapter_qa: bfloat16 [4, 1536, 16], replicated, may hold values from -0.15625 to 0.15625
- adapter_qb: bfloat16 [4, 16, 36864], replicated, may hold values from -0.29882812 to 0.29882812
- prefix_cache: bfloat16 [32768, 576], P('blk'), may hold values from -6 to 6
- prefix_mask: int32 [32, 256], P('batch', 'blk'), may hold values 0 or 1
- suffix_cache: bfloat16 [32, 4096, 576], P(('batch', 'blk')), may hold values from -6 to 6
- suffix_blocks: int32 [8, 4], P('blk'), may hold values from 1 to 32, 40 in all within a row
- new_latent: bfloat16 [32, 576], P(('batch', 'blk')), may hold values from -6 to 6
- value_up: bfloat16 [64, 512, 128], P('blk'), may hold values from -0.25 to 0.25
- out_weight: bfloat16 [8192, 7168], P('blk'), may hold values from -0.0625 to 0.0625
- adapter_oa: bfloat16 [4, 8192, 16], P(None, 'blk'), may hold values from -0.0625 to 0.0625
- adapter_ob: bfloat16 [4, 16, 7168], replicated, may hold values from -1.5 to 1.5
Outputs:
- attention_out: bfloat16 [32, 7168], P(('batch', 'blk'))
Inputs may be any that keep to these rules, and one draw needn't show every extreme that they name: `suffix_blocks`: each row holds 40 blocks in all, and its largest entry is exactly 32.
All inputs are finite; a program needn't handle non-finite values. No bound on the sum of `prefix_mask` on one device may be relied on, other than what follows from the above.
Results may differ from a plain program's by a relative error of at most 0.025.
Values may be sent and summed in bfloat16 or wider, within the bound.
A program may use at most 128 MiB of HBM per device.

v0:
```python
import jax
import jax.numpy as jnp
from jax import lax
from jax.sharding import PartitionSpec as P

D = 7168
H = 64
LAT = 512
QK = 192
RANK = 16
BLOCK = 128
KV = 576
floor_score = -1e30


def passed_along(block, axis, distance):
    devices = range(lax.axis_size(axis))
    route = [((i - distance) % len(devices), i) for i in devices]
    return lax.ppermute(block, axis, route)


def combine_parts(first_part, second_part):
    peak = jnp.maximum(first_part[0], second_part[0])
    first_scale = jnp.exp(first_part[0] - peak)
    second_scale = jnp.exp(second_part[0] - peak)
    totals = first_part[1] * first_scale + second_part[1] * second_scale
    sums = first_part[2] * first_scale[..., None] + second_part[2] * second_scale[..., None]
    return (peak, totals, sums)


def partial_softmax(scores, live_keys, values, per_row):
    masked = jnp.where(live_keys, scores, -jnp.inf)
    peak = jnp.maximum(jnp.max(masked, axis=-1), floor_score)
    weights = jnp.exp(masked - peak[..., None])
    totals = jnp.sum(weights, axis=-1)
    weights_low = weights.astype(jnp.bfloat16)
    if per_row:
        sums = jnp.einsum("nht,ntl->nhl", weights_low, values, preferred_element_type=jnp.float32)
    else:
        sums = jnp.einsum("nht,tl->nhl", weights_low, values, preferred_element_type=jnp.float32)
    return (peak, totals, sums)


def prefix_part(queries, mask_rows, prefix_cache, score_scale):
    count_rows = queries.shape[0]
    blocks_here = mask_rows.shape[1]
    scores = (
        jnp.einsum("nhk,tk->nht", queries, prefix_cache, preferred_element_type=jnp.float32)
        * score_scale
    )
    live_keys = jnp.broadcast_to((mask_rows > 0)[:, :, None], (count_rows, blocks_here, BLOCK))
    live_keys = live_keys.reshape(count_rows, 1, blocks_here * BLOCK)
    return partial_softmax(scores, live_keys, prefix_cache[:, :LAT], False)


def empty_parts(count_rows):
    return (
        jnp.full((count_rows, H), floor_score, jnp.float32),
        jnp.zeros((count_rows, H), jnp.float32),
        jnp.zeros((count_rows, H, LAT), jnp.float32),
    )


def on_device(
    query_base,
    query_latent,
    tenant_ids,
    adapter_qa,
    adapter_qb,
    prefix_cache,
    prefix_mask,
    suffix_cache,
    suffix_blocks,
    new_latent,
    value_up,
    out_weight,
    adapter_oa,
    adapter_ob,
):
    score_scale = QK ** (-0.5)
    blk_count = lax.axis_size("blk")
    blk_index = lax.axis_index("blk")
    batch_index = lax.axis_index("batch")
    owned_rows = query_base.shape[0]
    group_rows = owned_rows * blk_count
    tenants = adapter_qa.shape[0]
    own_tenant = lax.dynamic_slice_in_dim(tenant_ids, blk_index * owned_rows, owned_rows)
    tenant_hit = (own_tenant[:, None] == jnp.arange(tenants)[None, :]).astype(jnp.float32)
    low_every = jnp.einsum(
        "rq,tqk->rtk", query_latent, adapter_qa, preferred_element_type=jnp.float32
    )
    low_query = jnp.sum(low_every * tenant_hit[:, :, None], axis=1).astype(jnp.bfloat16)
    low_spread = (tenant_hit.astype(jnp.bfloat16)[:, :, None] * low_query[:, None, :]).reshape(
        owned_rows, tenants * RANK
    )
    delta_query = jnp.dot(
        low_spread, adapter_qb.reshape(tenants * RANK, H * KV), preferred_element_type=jnp.float32
    )
    query = (query_base.astype(jnp.float32) + delta_query).astype(jnp.bfloat16)
    query_heads = query.reshape(owned_rows, H, KV)

    def travel_step(visit_step, state):
        moving, running = state
        anchor = (blk_index - visit_step) % blk_count
        mask_rows = lax.dynamic_slice_in_dim(prefix_mask, anchor * owned_rows, owned_rows)
        fresh_part = prefix_part(
            moving.reshape(owned_rows, H, KV), mask_rows, prefix_cache, score_scale
        )
        running = combine_parts(running, fresh_part)
        moving = passed_along(moving, "blk", 1)
        running = passed_along((running[0], running[1], running[2]), "blk", 1)
        return (moving, running)

    final_state = lax.fori_loop(0, blk_count, travel_step, (query, empty_parts(owned_rows)))
    prefix_result = final_state[1]
    length_row = suffix_blocks[0]
    own_lengths = lax.dynamic_slice_in_dim(length_row, batch_index * owned_rows, owned_rows)
    slot_count = suffix_cache.shape[1]
    scores = (
        jnp.einsum("nhk,ntk->nht", query_heads, suffix_cache, preferred_element_type=jnp.float32)
        * score_scale
    )
    live_keys = jnp.arange(slot_count)[None, None, :] < (own_lengths * BLOCK)[:, None, None]
    suffix_result = partial_softmax(scores, live_keys, suffix_cache[:, :, :LAT], True)
    new_scores = (
        jnp.einsum("nhk,nk->nh", query_heads, new_latent, preferred_element_type=jnp.float32)
        * score_scale
    )
    new_values = jnp.broadcast_to(
        new_latent[:, None, :LAT].astype(jnp.float32), (owned_rows, H, LAT)
    )
    new_part = (new_scores, jnp.ones_like(new_scores), new_values)
    combined = combine_parts(combine_parts(prefix_result, suffix_result), new_part)
    context = (combined[2] / combined[1][..., None]).astype(jnp.bfloat16)
    head_rows = lax.all_to_all(context, "blk", split_axis=1, concat_axis=0, tiled=True)
    head_out = jnp.einsum("rhl,hlv->rhv", head_rows, value_up, preferred_element_type=jnp.float32)
    head_out = head_out.astype(jnp.bfloat16).reshape(group_rows, -1)
    group_hit = (tenant_ids[:, None] == jnp.arange(tenants)[None, :]).astype(jnp.float32)
    adapter_up = adapter_ob.reshape(tenants * RANK, D).astype(jnp.float32)
    projected = jnp.dot(head_out, out_weight, preferred_element_type=jnp.float32)
    low_every_out = jnp.einsum(
        "rk,tkj->rtj", head_out, adapter_oa, preferred_element_type=jnp.float32
    )
    low_spread_out = (low_every_out * group_hit[:, :, None]).reshape(
        lax.axis_size("blk") * owned_rows, tenants * RANK
    )
    return lax.psum_scatter(
        (projected + jnp.dot(low_spread_out, adapter_up, precision=lax.Precision.HIGHEST)).astype(
            jnp.bfloat16
        ),
        "blk",
        scatter_dimension=0,
        tiled=True,
    )


def solution(mesh):
    placed = (
        P(("batch", "blk"), None),
        P(("batch", "blk"), None),
        P("batch"),
        P(),
        P(),
        P("blk", None),
        P("batch", "blk"),
        P(("batch", "blk"), None, None),
        P("blk", None),
        P(("batch", "blk"), None),
        P("blk", None, None),
        P("blk", None),
        P(None, "blk", None),
        P(),
    )
    return jax.shard_map(
        on_device, mesh=mesh, in_specs=placed, out_specs=P(("batch", "blk"), None), check_vma=False
    )
```

profile of v0, /device:TPU:0, one launch (start us, length us, event | category | flops | bytes accessed | tf_op | source)
XLA Modules:
  0.0 224.7 jit_solution(18082579267390969847)
XLA Ops:
  6.5 1.4 dynamic_slice.16
  7.9 0.7 compare_convert_fusion
  8.6 1.3 fusion.63
  10.2 0.7 slice_convert_fusion
  10.9 1.3 fusion.81
  12.2 0.7 iota_compare_fusion
  12.9 3.2 %fusion.80 = (bf16[36864]{0:T(1024)(128)(2,1)S(1)}, bf16[1,36864]{1,0:T(2,128)(2,1)S(1)}) fusion(bf16[64,1]{0,1:T(2,128)(2,1)S(1)} %reshape.366, bf16[64,36864]{1,0:T(8,128)(2,1)} %bitcast.182, bf16[1,36864]{1,0:T(2,128)(2,1)} %param.16), kind=kOutput, calls=%fused_computation.86 | convolution fusion | flops 4829184 | bytes 4939904 | tf_op jit(solution)/shard_map/dot_general | solution.py:96
  16.2 3.5 %fusion.82 = (f32[64]{0:T(128)S(1)}, f32[64,4096]{1,0:T(8,128)S(1)}) fusion(bf16[64,576]{1,0:T(8,128)(2,1)S(1)} %reshape.358, bf16[1,4096,576]{1,2,0:T(8,128)(2,1)} %param.23, pred[4096]{0:T(1024)(128)(4,1)S(1)} %iota_compare_fusion), kind=kOutput, calls=%fused_computation.88 | convolution fusion | flops 302776256 | bytes 5845248 | tf_op jit(solution)/shard_map/nhk,ntk->nht/dot_general | solution.py:120
  20.0 0.6 broadcast_in_dim.84
  20.7 119.1 %while.21 = (s32[]{:T(128)}, bf16[1,36864]{1,0:T(2,128)(2,1)S(1)}, f32[1,64]{1,0:T(1,128)S(1)}, f32[1,64]{1,0:T(1,128)S(1)}, f32[1,64,512]{2,1,0:T(8,128)}, /*in...) while((s32[]{:T(128)}, bf16[1,36864]{1,0:T(2,128)(2,1)S(1)}, ...), condition=%wide.region_4.5_spmd, body=%wide.region_1.4_spmd.sunk | while | flops 572359104 | bytes 32546200 | solution.py:114
  20.7 0.7 compare_bitcast_fusion.2
  22.2 3.6 %fusion.109 = (f32[64]{0:T(128)S(1)}, f32[64,4096]{1,0:T(8,128)S(1)}) fusion(bf16[64,576]{1,0:T(8,128)(2,1)S(1)} %reshape.381, bf16[4096,576]{0,1:T(8,128)(2,1)} %get-tuple-element.336, pred[4096]{0:T(1024)(128)(4,1)S(1)} %broadcast_bitcast_fusion.2), kind=kOutput, calls=%fused_computation.85.clone.1 | convolution fusion | flops 302776256 | bytes 5845248 | tf_op jit(solution)/shard_map/while/body/eval_jaxpr/nhk,tk->nht/dot_general | solution.py:48
  26.2 2.3 %fusion.112 = f32[1,64,512]{2,1,0:T(8,128)S(1)} fusion(bf16[4096,576]{0,1:T(8,128)(2,1)S(1)} %copy-done.1, f32[64,4096]{1,0:T(8,128)S(1)} %get-tuple-element.298, f32[64]{0:T(128)S(1)} %broadcast_maximum_fusion.3, f32[1,64,512]{2,1,0:T(8,128)} %get-tuple-element.320, f32[64]{0:T(128)S(1)} %get-tuple-element.301, f32[64]{0:T(128)S(1)} %get-tuple-element.302), kind=kOutput, calls=%fused_computation.6.clone.1 | convolution fusion | flops 269058048 | bytes 5506560 | tf_op jit(solution)/shard_map/while/body/eval_jaxpr/nht,tl->nhl/dot_general | solution.py:40
  29.0 2.6 %collective-permute-start = (bf16[1,36864]{1,0:T(2,128)(2,1)S(1)}, bf16[1,36864]{1,0:T(2,128)(2,1)S(1)}, u32[]{:S(2)}, u32[]{:S(2)}) collective-permute-start(bf16[1,36864]{1,0:T(2,128)(2,1)S(1)} %copy.35), channel_id=1, source_target_pairs={{28,0},{0,4},{4,8},{8,12},{12,16},{16,20},{20,24},{24,28},{29,1},{... | collective-permute-start | bytes 221192 | tf_op jit(solution)/shard_map/while/body/eval_jaxpr/ppermute | solution.py:19
  31.6 1.5 collective-permute-start.2
  33.2 3.0 %collective-permute-done.1 = f32[1,64]{1,0:T(1,128)S(1)} collective-permute-done((f32[1,64]{1,0:T(1,128)S(1)}, f32[1,64]{1,0:T(1,128)S(1)}, u32[]{:S(2)}, u32[]{:S(2)}) %collective-permute-start.1) | collective-permute-done | bytes 288 | tf_op jit(solution)/shard_map/while/body/eval_jaxpr/ppermute | solution.py:19
  36.2 0.7 compare_bitcast_fusion.2
  37.7 3.6 %fusion.109 = (f32[64]{0:T(128)S(1)}, f32[64,4096]{1,0:T(8,128)S(1)}) fusion(bf16[64,576]{1,0:T(8,128)(2,1)S(1)} %reshape.381, bf16[4096,576]{0,1:T(8,128)(2,1)} %get-tuple-element.336, pred[4096]{0:T(1024)(128)(4,1)S(1)} %broadcast_bitcast_fusion.2), kind=kOutput, calls=%fused_computation.85.clone.1 | convolution fusion | flops 302776256 | bytes 5845248 | tf_op jit(solution)/shard_map/while/body/eval_jaxpr/nhk,tk->nht/dot_general | solution.py:48
  41.7 2.3 %fusion.112 = f32[1,64,512]{2,1,0:T(8,128)S(1)} fusion(bf16[4096,576]{0,1:T(8,128)(2,1)S(1)} %copy-done.1, f32[64,4096]{1,0:T(8,128)S(1)} %get-tuple-element.298, f32[64]{0:T(128)S(1)} %broadcast_maximum_fusion.3, f32[1,64,512]{2,1,0:T(8,128)} %get-tuple-element.320, f32[64]{0:T(128)S(1)} %get-tuple-element.301, f32[64]{0:T(128)S(1)} %get-tuple-element.302), kind=kOutput, calls=%fused_computation.6.clone.1 | convolution fusion | flops 269058048 | bytes 5506560 | tf_op jit(solution)/shard_map/while/body/eval_jaxpr/nht,tl->nhl/dot_general | solution.py:40
  44.1 1.4 collective-permute-start
  45.6 2.4 %collective-permute-start.2 = (f32[1,64]{1,0:T(1,128)S(1)}, f32[1,64]{1,0:T(1,128)S(1)}, u32[]{:S(2)}, u32[]{:S(2)}) collective-permute-start(f32[1,64]{1,0:T(1,128)S(1)} %get-tuple-element.300), channel_id=1, source_target_pairs={{28,0},{0,4},{4,8},{8,12},{12,16},{16,20},{20,24},{24,28},{29,1},{... | collective-permute-start | bytes 776 | tf_op jit(solution)/shard_map/while/body/eval_jaxpr/ppermute | solution.py:19
  48.0 3.0 %collective-permute-done.1 = f32[1,64]{1,0:T(1,128)S(1)} collective-permute-done((f32[1,64]{1,0:T(1,128)S(1)}, f32[1,64]{1,0:T(1,128)S(1)}, u32[]{:S(2)}, u32[]{:S(2)}) %collective-permute-start.1) | collective-permute-done | bytes 288 | tf_op jit(solution)/shard_map/while/body/eval_jaxpr/ppermute | solution.py:19
  51.0 0.7 compare_bitcast_fusion.2
  52.5 3.6 %fusion.109 = (f32[64]{0:T(128)S(1)}, f32[64,4096]{1,0:T(8,128)S(1)}) fusion(bf16[64,576]{1,0:T(8,128)(2,1)S(1)} %reshape.381, bf16[4096,576]{0,1:T(8,128)(2,1)} %get-tuple-element.336, pred[4096]{0:T(1024)(128)(4,1)S(1)} %broadcast_bitcast_fusion.2), kind=kOutput, calls=%fused_computation.85.clone.1 | convolution fusion | flops 302776256 | bytes 5845248 | tf_op jit(solution)/shard_map/while/body/eval_jaxpr/nhk,tk->nht/dot_general | solution.py:48
  56.5 2.3 %fusion.112 = f32[1,64,512]{2,1,0:T(8,128)S(1)} fusion(bf16[4096,576]{0,1:T(8,128)(2,1)S(1)} %copy-done.1, f32[64,4096]{1,0:T(8,128)S(1)} %get-tuple-element.298, f32[64]{0:T(128)S(1)} %broadcast_maximum_fusion.3, f32[1,64,512]{2,1,0:T(8,128)} %get-tuple-element.320, f32[64]{0:T(128)S(1)} %get-tuple-element.301, f32[64]{0:T(128)S(1)} %get-tuple-element.302), kind=kOutput, calls=%fused_computation.6.clone.1 | convolution fusion | flops 269058048 | bytes 5506560 | tf_op jit(solution)/shard_map/while/body/eval_jaxpr/nht,tl->nhl/dot_general | solution.py:40
  58.9 0.5 collective-permute-start
  59.5 3.3 %collective-permute-start.2 = (f32[1,64]{1,0:T(1,128)S(1)}, f32[1,64]{1,0:T(1,128)S(1)}, u32[]{:S(2)}, u32[]{:S(2)}) collective-permute-start(f32[1,64]{1,0:T(1,128)S(1)} %get-tuple-element.300), channel_id=1, source_target_pairs={{28,0},{0,4},{4,8},{8,12},{12,16},{16,20},{20,24},{24,28},{29,1},{... | collective-permute-start | bytes 776 | tf_op jit(solution)/shard_map/while/body/eval_jaxpr/ppermute | solution.py:19
  62.8 3.0 %collective-permute-done.1 = f32[1,64]{1,0:T(1,128)S(1)} collective-permute-done((f32[1,64]{1,0:T(1,128)S(1)}, f32[1,64]{1,0:T(1,128)S(1)}, u32[]{:S(2)}, u32[]{:S(2)}) %collective-permute-start.1) | collective-permute-done | bytes 288 | tf_op jit(solution)/shard_map/while/body/eval_jaxpr/ppermute | solution.py:19
  65.8 0.7 compare_bitcast_fusion.2
  67.3 3.6 %fusion.109 = (f32[64]{0:T(128)S(1)}, f32[64,4096]{1,0:T(8,128)S(1)}) fusion(bf16[64,576]{1,0:T(8,128)(2,1)S(1)} %reshape.381, bf16[4096,576]{0,1:T(8,128)(2,1)} %get-tuple-element.336, pred[4096]{0:T(1024)(128)(4,1)S(1)} %broadcast_bitcast_fusion.2), kind=kOutput, calls=%fused_computation.85.clone.1 | convolution fusion | flops 302776256 | bytes 5845248 | tf_op jit(solution)/shard_map/while/body/eval_jaxpr/nhk,tk->nht/dot_general | solution.py:48
  71.3 2.3 %fusion.112 = f32[1,64,512]{2,1,0:T(8,128)S(1)} fusion(bf16[4096,576]{0,1:T(8,128)(2,1)S(1)} %copy-done.1, f32[64,4096]{1,0:T(8,128)S(1)} %get-tuple-element.298, f32[64]{0:T(128)S(1)} %broadcast_maximum_fusion.3, f32[1,64,512]{2,1,0:T(8,128)} %get-tuple-element.320, f32[64]{0:T(128)S(1)} %get-tuple-element.301, f32[64]{0:T(128)S(1)} %get-tuple-element.302), kind=kOutput, calls=%fused_computation.6.clone.1 | convolution fusion | flops 269058048 | bytes 5506560 | tf_op jit(solution)/shard_map/while/body/eval_jaxpr/nht,tl->nhl/dot_general | solution.py:40
  74.2 3.4 %collective-permute-start.2 = (f32[1,64]{1,0:T(1,128)S(1)}, f32[1,64]{1,0:T(1,128)S(1)}, u32[]{:S(2)}, u32[]{:S(2)}) collective-permute-start(f32[1,64]{1,0:T(1,128)S(1)} %get-tuple-element.300), channel_id=1, source_target_pairs={{28,0},{0,4},{4,8},{8,12},{12,16},{16,20},{20,24},{24,28},{29,1},{... | collective-permute-start | bytes 776 | tf_op jit(solution)/shard_map/while/body/eval_jaxpr/ppermute | solution.py:19
  77.6 3.0 %collective-permute-done.1 = f32[1,64]{1,0:T(1,128)S(1)} collective-permute-done((f32[1,64]{1,0:T(1,128)S(1)}, f32[1,64]{1,0:T(1,128)S(1)}, u32[]{:S(2)}, u32[]{:S(2)}) %collective-permute-start.1) | collective-permute-done | bytes 288 | tf_op jit(solution)/shard_map/while/body/eval_jaxpr/ppermute | solution.py:19
  80.6 0.7 compare_bitcast_fusion.2
  82.1 3.6 %fusion.109 = (f32[64]{0:T(128)S(1)}, f32[64,4096]{1,0:T(8,128)S(1)}) fusion(bf16[64,576]{1,0:T(8,128)(2,1)S(1)} %reshape.381, bf16[4096,576]{0,1:T(8,128)(2,1)} %get-tuple-element.336, pred[4096]{0:T(1024)(128)(4,1)S(1)} %broadcast_bitcast_fusion.2), kind=kOutput, calls=%fused_computation.85.clone.1 | convolution fusion | flops 302776256 | bytes 5845248 | tf_op jit(solution)/shard_map/while/body/eval_jaxpr/nhk,tk->nht/dot_general | solution.py:48
  86.1 2.3 %fusion.112 = f32[1,64,512]{2,1,0:T(8,128)S(1)} fusion(bf16[4096,576]{0,1:T(8,128)(2,1)S(1)} %copy-done.1, f32[64,4096]{1,0:T(8,128)S(1)} %get-tuple-element.298, f32[64]{0:T(128)S(1)} %broadcast_maximum_fusion.3, f32[1,64,512]{2,1,0:T(8,128)} %get-tuple-element.320, f32[64]{0:T(128)S(1)} %get-tuple-element.301, f32[64]{0:T(128)S(1)} %get-tuple-element.302), kind=kOutput, calls=%fused_computation.6.clone.1 | convolution fusion | flops 269058048 | bytes 5506560 | tf_op jit(solution)/shard_map/while/body/eval_jaxpr/nht,tl->nhl/dot_general | solution.py:40
  89.0 3.4 %collective-permute-start.2 = (f32[1,64]{1,0:T(1,128)S(1)}, f32[1,64]{1,0:T(1,128)S(1)}, u32[]{:S(2)}, u32[]{:S(2)}) collective-permute-start(f32[1,64]{1,0:T(1,128)S(1)} %get-tuple-element.300), channel_id=1, source_target_pairs={{28,0},{0,4},{4,8},{8,12},{12,16},{16,20},{20,24},{24,28},{29,1},{... | collective-permute-start | bytes 776 | tf_op jit(solution)/shard_map/while/body/eval_jaxpr/ppermute | solution.py:19
  92.4 3.0 %collective-permute-done.1 = f32[1,64]{1,0:T(1,128)S(1)} collective-permute-done((f32[1,64]{1,0:T(1,128)S(1)}, f32[1,64]{1,0:T(1,128)S(1)}, u32[]{:S(2)}, u32[]{:S(2)}) %collective-permute-start.1) | collective-permute-done | bytes 288 | tf_op jit(solution)/shard_map/while/body/eval_jaxpr/ppermute | solution.py:19
  95.4 0.7 compare_bitcast_fusion.2
  96.9 3.6 %fusion.109 = (f32[64]{0:T(128)S(1)}, f32[64,4096]{1,0:T(8,128)S(1)}) fusion(bf16[64,576]{1,0:T(8,128)(2,1)S(1)} %reshape.381, bf16[4096,576]{0,1:T(8,128)(2,1)} %get-tuple-element.336, pred[4096]{0:T(1024)(128)(4,1)S(1)} %broadcast_bitcast_fusion.2), kind=kOutput, calls=%fused_computation.85.clone.1 | convolution fusion | flops 302776256 | bytes 5845248 | tf_op jit(solution)/shard_map/while/body/eval_jaxpr/nhk,tk->nht/dot_general | solution.py:48
  100.9 2.3 %fusion.112 = f32[1,64,512]{2,1,0:T(8,128)S(1)} fusion(bf16[4096,576]{0,1:T(8,128)(2,1)S(1)} %copy-done.1, f32[64,4096]{1,0:T(8,128)S(1)} %get-tuple-element.298, f32[64]{0:T(128)S(1)} %broadcast_maximum_fusion.3, f32[1,64,512]{2,1,0:T(8,128)} %get-tuple-element.320, f32[64]{0:T(128)S(1)} %get-tuple-element.301, f32[64]{0:T(128)S(1)} %get-tuple-element.302), kind=kOutput, calls=%fused_computation.6.clone.1 | convolution fusion | flops 269058048 | bytes 5506560 | tf_op jit(solution)/shard_map/while/body/eval_jaxpr/nht,tl->nhl/dot_general | solution.py:40
  103.8 3.4 %collective-permute-start.2 = (f32[1,64]{1,0:T(1,128)S(1)}, f32[1,64]{1,0:T(1,128)S(1)}, u32[]{:S(2)}, u32[]{:S(2)}) collective-permute-start(f32[1,64]{1,0:T(1,128)S(1)} %get-tuple-element.300), channel_id=1, source_target_pairs={{28,0},{0,4},{4,8},{8,12},{12,16},{16,20},{20,24},{24,28},{29,1},{... | collective-permute-start | bytes 776 | tf_op jit(solution)/shard_map/while/body/eval_jaxpr/ppermute | solution.py:19
  107.2 3.0 %collective-permute-done.1 = f32[1,64]{1,0:T(1,128)S(1)} collective-permute-done((f32[1,64]{1,0:T(1,128)S(1)}, f32[1,64]{1,0:T(1,128)S(1)}, u32[]{:S(2)}, u32[]{:S(2)}) %collective-permute-start.1) | collective-permute-done | bytes 288 | tf_op jit(solution)/shard_map/while/body/eval_jaxpr/ppermute | solution.py:19
  110.3 0.7 compare_bitcast_fusion.2
  111.7 3.6 %fusion.109 = (f32[64]{0:T(128)S(1)}, f32[64,4096]{1,0:T(8,128)S(1)}) fusion(bf16[64,576]{1,0:T(8,128)(2,1)S(1)} %reshape.381, bf16[4096,576]{0,1:T(8,128)(2,1)} %get-tuple-element.336, pred[4096]{0:T(1024)(128)(4,1)S(1)} %broadcast_bitcast_fusion.2), kind=kOutput, calls=%fused_computation.85.clone.1 | convolution fusion | flops 302776256 | bytes 5845248 | tf_op jit(solution)/shard_map/while/body/eval_jaxpr/nhk,tk->nht/dot_general | solution.py:48
  115.7 2.3 %fusion.112 = f32[1,64,512]{2,1,0:T(8,128)S(1)} fusion(bf16[4096,576]{0,1:T(8,128)(2,1)S(1)} %copy-done.1, f32[64,4096]{1,0:T(8,128)S(1)} %get-tuple-element.298, f32[64]{0:T(128)S(1)} %broadcast_maximum_fusion.3, f32[1,64,512]{2,1,0:T(8,128)} %get-tuple-element.320, f32[64]{0:T(128)S(1)} %get-tuple-element.301, f32[64]{0:T(128)S(1)} %get-tuple-element.302), kind=kOutput, calls=%fused_computation.6.clone.1 | convolution fusion | flops 269058048 | bytes 5506560 | tf_op jit(solution)/shard_map/while/body/eval_jaxpr/nht,tl->nhl/dot_general | solution.py:40
  118.6 3.4 %collective-permute-start.2 = (f32[1,64]{1,0:T(1,128)S(1)}, f32[1,64]{1,0:T(1,128)S(1)}, u32[]{:S(2)}, u32[]{:S(2)}) collective-permute-start(f32[1,64]{1,0:T(1,128)S(1)} %get-tuple-element.300), channel_id=1, source_target_pairs={{28,0},{0,4},{4,8},{8,12},{12,16},{16,20},{20,24},{24,28},{29,1},{... | collective-permute-start | bytes 776 | tf_op jit(solution)/shard_map/while/body/eval_jaxpr/ppermute | solution.py:19
  122.0 3.0 %collective-permute-done.1 = f32[1,64]{1,0:T(1,128)S(1)} collective-permute-done((f32[1,64]{1,0:T(1,128)S(1)}, f32[1,64]{1,0:T(1,128)S(1)}, u32[]{:S(2)}, u32[]{:S(2)}) %collective-permute-start.1) | collective-permute-done | bytes 288 | tf_op jit(solution)/shard_map/while/body/eval_jaxpr/ppermute | solution.py:19
  125.1 0.7 compare_bitcast_fusion.2
  126.5 3.6 %fusion.109 = (f32[64]{0:T(128)S(1)}, f32[64,4096]{1,0:T(8,128)S(1)}) fusion(bf16[64,576]{1,0:T(8,128)(2,1)S(1)} %reshape.381, bf16[4096,576]{0,1:T(8,128)(2,1)} %get-tuple-element.336, pred[4096]{0:T(1024)(128)(4,1)S(1)} %broadcast_bitcast_fusion.2), kind=kOutput, calls=%fused_computation.85.clone.1 | convolution fusion | flops 302776256 | bytes 5845248 | tf_op jit(solution)/shard_map/while/body/eval_jaxpr/nhk,tk->nht/dot_general | solution.py:48
  130.5 2.3 %fusion.112 = f32[1,64,512]{2,1,0:T(8,128)S(1)} fusion(bf16[4096,576]{0,1:T(8,128)(2,1)S(1)} %copy-done.1, f32[64,4096]{1,0:T(8,128)S(1)} %get-tuple-element.298, f32[64]{0:T(128)S(1)} %broadcast_maximum_fusion.3, f32[1,64,512]{2,1,0:T(8,128)} %get-tuple-element.320, f32[64]{0:T(128)S(1)} %get-tuple-element.301, f32[64]{0:T(128)S(1)} %get-tuple-element.302), kind=kOutput, calls=%fused_computation.6.clone.1 | convolution fusion | flops 269058048 | bytes 5506560 | tf_op jit(solution)/shard_map/while/body/eval_jaxpr/nht,tl->nhl/dot_general | solution.py:40
  133.4 3.4 %collective-permute-start.2 = (f32[1,64]{1,0:T(1,128)S(1)}, f32[1,64]{1,0:T(1,128)S(1)}, u32[]{:S(2)}, u32[]{:S(2)}) collective-permute-start(f32[1,64]{1,0:T(1,128)S(1)} %get-tuple-element.300), channel_id=1, source_target_pairs={{28,0},{0,4},{4,8},{8,12},{12,16},{16,20},{20,24},{24,28},{29,1},{... | collective-permute-start | bytes 776 | tf_op jit(solution)/shard_map/while/body/eval_jaxpr/ppermute | solution.py:19
  136.8 3.0 %collective-permute-done.1 = f32[1,64]{1,0:T(1,128)S(1)} collective-permute-done((f32[1,64]{1,0:T(1,128)S(1)}, f32[1,64]{1,0:T(1,128)S(1)}, u32[]{:S(2)}, u32[]{:S(2)}) %collective-permute-start.1) | collective-permute-done | bytes 288 | tf_op jit(solution)/shard_map/while/body/eval_jaxpr/ppermute | solution.py:19
  140.0 3.8 %fusion.53 = bf16[1,64,512]{2,1,0:T(8,128)(2,1)S(1)} fusion(bf16[1,4096,576]{1,2,0:T(8,128)(2,1)} %param.23, f32[64,4096]{1,0:T(8,128)S(1)} %get-tuple-element.239, f32[64]{0:T(128)S(1)} %broadcast_maximum_fusion.1, f32[1,64,512]{2,1,0:T(8,128)} %get-tuple-element.206, f32[64]{0:T(128)S(1)} %get-tuple-element.232, f32[64]{0:T(128)S(1)} %get-tuple-element.233, ...), kind=kOutput, calls=%fused_computation.45 | convolution fusion | flops 269221888 | bytes 5443072 | tf_op jit(solution)/shard_map/nht,ntl->nhl/dot_general | solution.py:38
  143.9 0.5 broadcast.272
  144.4 1.0 reduce.23
  145.5 0.7 reshape.378
  146.1 3.5 %all-to-all-start = ((bf16[8,2,2048]{2,1,0:T(2,128)(2,1)}), bf16[8,2,2048]{2,1,0:T(2,128)(2,1)S(1)}, u32[]{:S(2)}, u32[]{:S(2)}) async-start(bf16[8,2,2048]{2,1,0:T(2,128)(2,1)} %reshape.378), calls=%async_computation | async-start | bytes 131072 | tf_op jit(solution)/shard_map/all_to_all | solution.py:135
  149.7 5.0 %all-to-all-done = bf16[8,2,2048]{2,1,0:T(2,128)(2,1)S(1)} async-done(((bf16[8,2,2048]{2,1,0:T(2,128)(2,1)}), bf16[8,2,2048]{2,1,0:T(2,128)(2,1)S(1)}, u32[]{:S(2)}, u32[]{:S(2)}) %all-to-all-start) | async-done | bytes 65568 | tf_op jit(solution)/shard_map/all_to_all | solution.py:135
  155.3 1.1 convolution_bitcast_fusion
  156.3 7.8 %fusion.21 = bf16[8,7168]{1,0:T(8,128)(2,1)} fusion(f32[8,7168]{1,0:T(8,128)S(1)} %convolution_bitcast_fusion, bf16[1024,7168]{1,0:T(8,128)(2,1)} %param.27, bf16[8,8,128]{2,1,0:T(8,128)(2,1)S(1)} %convolution_convert_fusion), kind=kOutput, calls=%fused_computation.26 | convolution fusion | flops 117555200 | bytes 15040512 | tf_op jit(solution)/shard_map/dot_general | solution.py:140
  164.2 0.6 dynamic-slice.1
  164.8 50.9 %all-reduce.3.cloned.1.call-done = bf16[8,7168]{1,0:T(8,128)(2,1)} async-done(((bf16[8,7168]{1,0:T(8,128)(2,1)}), bf16[8,7168]{1,0:T(8,128)(2,1)}) %all-reduce.3.cloned.1.call-update) | async-done | bytes 114704
  215.8 2.1 constant_dynamic-slice_fusion
  (146 shorter events, 14.4 us)
Async XLA Ops:
  6.5 148.2 %copy-start = (bf16[8,512,128]{2,1,0:T(8,128)(2,1)S(1)}, bf16[8,512,128]{2,1,0:T(8,128)(2,1)}, u32[]{:S(2)}) copy-start(bf16[8,512,128]{2,1,0:T(8,128)(2,1)} %param.26) | copy-start | bytes 3145732
  20.7 119.2 %copy-start.3 = (bf16[1,576]{1,0:T(2,128)(2,1)S(1)}, bf16[1,576]{1,0:T(2,128)(2,1)}, u32[]{:S(2)}) copy-start(bf16[1,576]{1,0:T(2,128)(2,1)} %param.25) | copy-start | bytes 3460
  22.2 4.0 %copy-start.1 = (bf16[4096,576]{0,1:T(8,128)(2,1)S(1)}, bf16[4096,576]{0,1:T(8,128)(2,1)}, u32[]{:S(2)}) copy-start(bf16[4096,576]{0,1:T(8,128)(2,1)} %get-tuple-element.336) | copy-start | bytes 14155780 | tf_op jit(solution)/shard_map/while
  28.5 7.7 %collective-permute-start.3 = (f32[1,64,512]{2,1,0:T(8,128)S(1)}, f32[1,64,512]{2,1,0:T(8,128)}, u32[]{:S(2)}, u32[]{:S(2)}) collective-permute-start(f32[1,64,512]{2,1,0:T(8,128)S(1)} %fusion.112), channel_id=1, source_target_pairs={{28,0},{0,4},{4,8},{8,12},{12,16},{16,20},{20,24},{24,28},{29,1},{... | collective-permute-start | bytes 393224 | tf_op jit(solution)/shard_map/while/body/eval_jaxpr/ppermute | solution.py:19
  29.0 7.2 %collective-permute-start = (bf16[1,36864]{1,0:T(2,128)(2,1)S(1)}, bf16[1,36864]{1,0:T(2,128)(2,1)S(1)}, u32[]{:S(2)}, u32[]{:S(2)}) collective-permute-start(bf16[1,36864]{1,0:T(2,128)(2,1)S(1)} %copy.35), channel_id=1, source_target_pairs={{28,0},{0,4},{4,8},{8,12},{12,16},{16,20},{20,24},{24,28},{29,1},{... | collective-permute-start | bytes 221192 | tf_op jit(solution)/shard_map/while/body/eval_jaxpr/ppermute | solution.py:19
  31.6 4.6 %collective-permute-start.1 = (f32[1,64]{1,0:T(1,128)S(1)}, f32[1,64]{1,0:T(1,128)S(1)}, u32[]{:S(2)}, u32[]{:S(2)}) collective-permute-start(f32[1,64]{1,0:T(1,128)S(1)} %get-tuple-element.299), channel_id=1, source_target_pairs={{28,0},{0,4},{4,8},{8,12},{12,16},{16,20},{20,24},{24,28},{29,1},{... | collective-permute-start | bytes 776 | tf_op jit(solution)/shard_map/while/body/eval_jaxpr/ppermute | solution.py:19
  31.6 4.5 %collective-permute-start.2 = (f32[1,64]{1,0:T(1,128)S(1)}, f32[1,64]{1,0:T(1,128)S(1)}, u32[]{:S(2)}, u32[]{:S(2)}) collective-permute-start(f32[1,64]{1,0:T(1,128)S(1)} %get-tuple-element.300), channel_id=1, source_target_pairs={{28,0},{0,4},{4,8},{8,12},{12,16},{16,20},{20,24},{24,28},{29,1},{... | collective-permute-start | bytes 776 | tf_op jit(solution)/shard_map/while/body/eval_jaxpr/ppermute | solution.py:19
  37.7 4.0 %copy-start.1 = (bf16[4096,576]{0,1:T(8,128)(2,1)S(1)}, bf16[4096,576]{0,1:T(8,128)(2,1)}, u32[]{:S(2)}) copy-start(bf16[4096,576]{0,1:T(8,128)(2,1)} %get-tuple-element.336) | copy-start | bytes 14155780 | tf_op jit(solution)/shard_map/while
  44.0 7.0 %collective-permute-start.3 = (f32[1,64,512]{2,1,0:T(8,128)S(1)}, f32[1,64,512]{2,1,0:T(8,128)}, u32[]{:S(2)}, u32[]{:S(2)}) collective-permute-start(f32[1,64,512]{2,1,0:T(8,128)S(1)} %fusion.112), channel_id=1, source_target_pairs={{28,0},{0,4},{4,8},{8,12},{12,16},{16,20},{20,24},{24,28},{29,1},{... | collective-permute-start | bytes 393224 | tf_op jit(solution)/shard_map/while/body/eval_jaxpr/ppermute | solution.py:19
  44.1 6.9 %collective-permute-start = (bf16[1,36864]{1,0:T(2,128)(2,1)S(1)}, bf16[1,36864]{1,0:T(2,128)(2,1)S(1)}, u32[]{:S(2)}, u32[]{:S(2)}) collective-permute-start(bf16[1,36864]{1,0:T(2,128)(2,1)S(1)} %copy.35), channel_id=1, source_target_pairs={{28,0},{0,4},{4,8},{8,12},{12,16},{16,20},{20,24},{24,28},{29,1},{... | collective-permute-start | bytes 221192 | tf_op jit(solution)/shard_map/while/body/eval_jaxpr/ppermute | solution.py:19
  45.5 5.5 %collective-permute-start.1 = (f32[1,64]{1,0:T(1,128)S(1)}, f32[1,64]{1,0:T(1,128)S(1)}, u32[]{:S(2)}, u32[]{:S(2)}) collective-permute-start(f32[1,64]{1,0:T(1,128)S(1)} %get-tuple-element.299), channel_id=1, source_target_pairs={{28,0},{0,4},{4,8},{8,12},{12,16},{16,20},{20,24},{24,28},{29,1},{... | collective-permute-start | bytes 776 | tf_op jit(solution)/shard_map/while/body/eval_jaxpr/ppermute | solution.py:19
  45.6 5.4 %collective-permute-start.2 = (f32[1,64]{1,0:T(1,128)S(1)}, f32[1,64]{1,0:T(1,128)S(1)}, u32[]{:S(2)}, u32[]{:S(2)}) collective-permute-start(f32[1,64]{1,0:T(1,128)S(1)} %get-tuple-element.300), channel_id=1, source_target_pairs={{28,0},{0,4},{4,8},{8,12},{12,16},{16,20},{20,24},{24,28},{29,1},{... | collective-permute-start | bytes 776 | tf_op jit(solution)/shard_map/while/body/eval_jaxpr/ppermute | solution.py:19
  52.5 4.0 %copy-start.1 = (bf16[4096,576]{0,1:T(8,128)(2,1)S(1)}, bf16[4096,576]{0,1:T(8,128)(2,1)}, u32[]{:S(2)}) copy-start(bf16[4096,576]{0,1:T(8,128)(2,1)} %get-tuple-element.336) | copy-start | bytes 14155780 | tf_op jit(solution)/shard_map/while
  58.8 7.0 %collective-permute-start.3 = (f32[1,64,512]{2,1,0:T(8,128)S(1)}, f32[1,64,512]{2,1,0:T(8,128)}, u32[]{:S(2)}, u32[]{:S(2)}) collective-permute-start(f32[1,64,512]{2,1,0:T(8,128)S(1)} %fusion.112), channel_id=1, source_target_pairs={{28,0},{0,4},{4,8},{8,12},{12,16},{16,20},{20,24},{24,28},{29,1},{... | collective-permute-start | bytes 393224 | tf_op jit(solution)/shard_map/while/body/eval_jaxpr/ppermute | solution.py:19
  58.9 6.9 %collective-permute-start = (bf16[1,36864]{1,0:T(2,128)(2,1)S(1)}, bf16[1,36864]{1,0:T(2,128)(2,1)S(1)}, u32[]{:S(2)}, u32[]{:S(2)}) collective-permute-start(bf16[1,36864]{1,0:T(2,128)(2,1)S(1)} %copy.35), channel_id=1, source_target_pairs={{28,0},{0,4},{4,8},{8,12},{12,16},{16,20},{20,24},{24,28},{29,1},{... | collective-permute-start | bytes 221192 | tf_op jit(solution)/shard_map/while/body/eval_jaxpr/ppermute | solution.py:19
  59.4 6.4 %collective-permute-start.1 = (f32[1,64]{1,0:T(1,128)S(1)}, f32[1,64]{1,0:T(1,128)S(1)}, u32[]{:S(2)}, u32[]{:S(2)}) collective-permute-start(f32[1,64]{1,0:T(1,128)S(1)} %get-tuple-element.299), channel_id=1, source_target_pairs={{28,0},{0,4},{4,8},{8,12},{12,16},{16,20},{20,24},{24,28},{29,1},{... | collective-permute-start | bytes 776 | tf_op jit(solution)/shard_map/while/body/eval_jaxpr/ppermute | solution.py:19
  59.5 6.3 %collective-permute-start.2 = (f32[1,64]{1,0:T(1,128)S(1)}, f32[1,64]{1,0:T(1,128)S(1)}, u32[]{:S(2)}, u32[]{:S(2)}) collective-permute-start(f32[1,64]{1,0:T(1,128)S(1)} %get-tuple-element.300), channel_id=1, source_target_pairs={{28,0},{0,4},{4,8},{8,12},{12,16},{16,20},{20,24},{24,28},{29,1},{... | collective-permute-start | bytes 776 | tf_op jit(solution)/shard_map/while/body/eval_jaxpr/ppermute | solution.py:19
  67.3 4.0 %copy-start.1 = (bf16[4096,576]{0,1:T(8,128)(2,1)S(1)}, bf16[4096,576]{0,1:T(8,128)(2,1)}, u32[]{:S(2)}) copy-start(bf16[4096,576]{0,1:T(8,128)(2,1)} %get-tuple-element.336) | copy-start | bytes 14155780 | tf_op jit(solution)/shard_map/while
  73.6 7.0 %collective-permute-start.3 = (f32[1,64,512]{2,1,0:T(8,128)S(1)}, f32[1,64,512]{2,1,0:T(8,128)}, u32[]{:S(2)}, u32[]{:S(2)}) collective-permute-start(f32[1,64,512]{2,1,0:T(8,128)S(1)} %fusion.112), channel_id=1, source_target_pairs={{28,0},{0,4},{4,8},{8,12},{12,16},{16,20},{20,24},{24,28},{29,1},{... | collective-permute-start | bytes 393224 | tf_op jit(solution)/shard_map/while/body/eval_jaxpr/ppermute | solution.py:19
  73.7 6.9 %collective-permute-start = (bf16[1,36864]{1,0:T(2,128)(2,1)S(1)}, bf16[1,36864]{1,0:T(2,128)(2,1)S(1)}, u32[]{:S(2)}, u32[]{:S(2)}) collective-permute-start(bf16[1,36864]{1,0:T(2,128)(2,1)S(1)} %copy.35), channel_id=1, source_target_pairs={{28,0},{0,4},{4,8},{8,12},{12,16},{16,20},{20,24},{24,28},{29,1},{... | collective-permute-start | bytes 221192 | tf_op jit(solution)/shard_map/while/body/eval_jaxpr/ppermute | solution.py:19
  73.7 6.8 %collective-permute-start.1 = (f32[1,64]{1,0:T(1,128)S(1)}, f32[1,64]{1,0:T(1,128)S(1)}, u32[]{:S(2)}, u32[]{:S(2)}) collective-permute-start(f32[1,64]{1,0:T(1,128)S(1)} %get-tuple-element.299), channel_id=1, source_target_pairs={{28,0},{0,4},{4,8},{8,12},{12,16},{16,20},{20,24},{24,28},{29,1},{... | collective-permute-start | bytes 776 | tf_op jit(solution)/shard_map/while/body/eval_jaxpr/ppermute | solution.py:19
  74.2 6.4 %collective-permute-start.2 = (f32[1,64]{1,0:T(1,128)S(1)}, f32[1,64]{1,0:T(1,128)S(1)}, u32[]{:S(2)}, u32[]{:S(2)}) collective-permute-start(f32[1,64]{1,0:T(1,128)S(1)} %get-tuple-element.300), channel_id=1, source_target_pairs={{28,0},{0,4},{4,8},{8,12},{12,16},{16,20},{20,24},{24,28},{29,1},{... | collective-permute-start | bytes 776 | tf_op jit(solution)/shard_map/while/body/eval_jaxpr/ppermute | solution.py:19
  82.1 4.0 %copy-start.1 = (bf16[4096,576]{0,1:T(8,128)(2,1)S(1)}, bf16[4096,576]{0,1:T(8,128)(2,1)}, u32[]{:S(2)}) copy-start(bf16[4096,576]{0,1:T(8,128)(2,1)} %get-tuple-element.336) | copy-start | bytes 14155780 | tf_op jit(solution)/shard_map/while
  88.4 7.0 %collective-permute-start.3 = (f32[1,64,512]{2,1,0:T(8,128)S(1)}, f32[1,64,512]{2,1,0:T(8,128)}, u32[]{:S(2)}, u32[]{:S(2)}) collective-permute-start(f32[1,64,512]{2,1,0:T(8,128)S(1)} %fusion.112), channel_id=1, source_target_pairs={{28,0},{0,4},{4,8},{8,12},{12,16},{16,20},{20,24},{24,28},{29,1},{... | collective-permute-start | bytes 393224 | tf_op jit(solution)/shard_map/while/body/eval_jaxpr/ppermute | solution.py:19
  88.5 6.9 %collective-permute-start = (bf16[1,36864]{1,0:T(2,128)(2,1)S(1)}, bf16[1,36864]{1,0:T(2,128)(2,1)S(1)}, u32[]{:S(2)}, u32[]{:S(2)}) collective-permute-start(bf16[1,36864]{1,0:T(2,128)(2,1)S(1)} %copy.35), channel_id=1, source_target_pairs={{28,0},{0,4},{4,8},{8,12},{12,16},{16,20},{20,24},{24,28},{29,1},{... | collective-permute-start | bytes 221192 | tf_op jit(solution)/shard_map/while/body/eval_jaxpr/ppermute | solution.py:19
  88.6 6.8 %collective-permute-start.1 = (f32[1,64]{1,0:T(1,128)S(1)}, f32[1,64]{1,0:T(1,128)S(1)}, u32[]{:S(2)}, u32[]{:S(2)}) collective-permute-start(f32[1,64]{1,0:T(1,128)S(1)} %get-tuple-element.299), channel_id=1, source_target_pairs={{28,0},{0,4},{4,8},{8,12},{12,16},{16,20},{20,24},{24,28},{29,1},{... | collective-permute-start | bytes 776 | tf_op jit(solution)/shard_map/while/body/eval_jaxpr/ppermute | solution.py:19
  89.0 6.4 %collective-permute-start.2 = (f32[1,64]{1,0:T(1,128)S(1)}, f32[1,64]{1,0:T(1,128)S(1)}, u32[]{:S(2)}, u32[]{:S(2)}) collective-permute-start(f32[1,64]{1,0:T(1,128)S(1)} %get-tuple-element.300), channel_id=1, source_target_pairs={{28,0},{0,4},{4,8},{8,12},{12,16},{16,20},{20,24},{24,28},{29,1},{... | collective-permute-start | bytes 776 | tf_op jit(solution)/shard_map/while/body/eval_jaxpr/ppermute | solution.py:19
  96.9 4.0 %copy-start.1 = (bf16[4096,576]{0,1:T(8,128)(2,1)S(1)}, bf16[4096,576]{0,1:T(8,128)(2,1)}, u32[]{:S(2)}) copy-start(bf16[4096,576]{0,1:T(8,128)(2,1)} %get-tuple-element.336) | copy-start | bytes 14155780 | tf_op jit(solution)/shard_map/while
  103.2 7.0 %collective-permute-start.3 = (f32[1,64,512]{2,1,0:T(8,128)S(1)}, f32[1,64,512]{2,1,0:T(8,128)}, u32[]{:S(2)}, u32[]{:S(2)}) collective-permute-start(f32[1,64,512]{2,1,0:T(8,128)S(1)} %fusion.112), channel_id=1, source_target_pairs={{28,0},{0,4},{4,8},{8,12},{12,16},{16,20},{20,24},{24,28},{29,1},{... | collective-permute-start | bytes 393224 | tf_op jit(solution)/shard_map/while/body/eval_jaxpr/ppermute | solution.py:19
  103.3 6.9 %collective-permute-start = (bf16[1,36864]{1,0:T(2,128)(2,1)S(1)}, bf16[1,36864]{1,0:T(2,128)(2,1)S(1)}, u32[]{:S(2)}, u32[]{:S(2)}) collective-permute-start(bf16[1,36864]{1,0:T(2,128)(2,1)S(1)} %copy.35), channel_id=1, source_target_pairs={{28,0},{0,4},{4,8},{8,12},{12,16},{16,20},{20,24},{24,28},{29,1},{... | collective-permute-start | bytes 221192 | tf_op jit(solution)/shard_map/while/body/eval_jaxpr/ppermute | solution.py:19
  103.4 6.8 %collective-permute-start.1 = (f32[1,64]{1,0:T(1,128)S(1)}, f32[1,64]{1,0:T(1,128)S(1)}, u32[]{:S(2)}, u32[]{:S(2)}) collective-permute-start(f32[1,64]{1,0:T(1,128)S(1)} %get-tuple-element.299), channel_id=1, source_target_pairs={{28,0},{0,4},{4,8},{8,12},{12,16},{16,20},{20,24},{24,28},{29,1},{... | collective-permute-start | bytes 776 | tf_op jit(solution)/shard_map/while/body/eval_jaxpr/ppermute | solution.py:19
  103.8 6.4 %collective-permute-start.2 = (f32[1,64]{1,0:T(1,128)S(1)}, f32[1,64]{1,0:T(1,128)S(1)}, u32[]{:S(2)}, u32[]{:S(2)}) collective-permute-start(f32[1,64]{1,0:T(1,128)S(1)} %get-tuple-element.300), channel_id=1, source_target_pairs={{28,0},{0,4},{4,8},{8,12},{12,16},{16,20},{20,24},{24,28},{29,1},{... | collective-permute-start | bytes 776 | tf_op jit(solution)/shard_map/while/body/eval_jaxpr/ppermute | solution.py:19
  111.7 4.0 %copy-start.1 = (bf16[4096,576]{0,1:T(8,128)(2,1)S(1)}, bf16[4096,576]{0,1:T(8,128)(2,1)}, u32[]{:S(2)}) copy-start(bf16[4096,576]{0,1:T(8,128)(2,1)} %get-tuple-element.336) | copy-start | bytes 14155780 | tf_op jit(solution)/shard_map/while
  118.0 7.0 %collective-permute-start.3 = (f32[1,64,512]{2,1,0:T(8,128)S(1)}, f32[1,64,512]{2,1,0:T(8,128)}, u32[]{:S(2)}, u32[]{:S(2)}) collective-permute-start(f32[1,64,512]{2,1,0:T(8,128)S(1)} %fusion.112), channel_id=1, source_target_pairs={{28,0},{0,4},{4,8},{8,12},{12,16},{16,20},{20,24},{24,28},{29,1},{... | collective-permute-start | bytes 393224 | tf_op jit(solution)/shard_map/while/body/eval_jaxpr/ppermute | solution.py:19
  118.1 6.9 %collective-permute-start = (bf16[1,36864]{1,0:T(2,128)(2,1)S(1)}, bf16[1,36864]{1,0:T(2,128)(2,1)S(1)}, u32[]{:S(2)}, u32[]{:S(2)}) collective-permute-start(bf16[1,36864]{1,0:T(2,128)(2,1)S(1)} %copy.35), channel_id=1, source_target_pairs={{28,0},{0,4},{4,8},{8,12},{12,16},{16,20},{20,24},{24,28},{29,1},{... | collective-permute-start | bytes 221192 | tf_op jit(solution)/shard_map/while/body/eval_jaxpr/ppermute | solution.py:19
  118.2 6.8 %collective-permute-start.1 = (f32[1,64]{1,0:T(1,128)S(1)}, f32[1,64]{1,0:T(1,128)S(1)}, u32[]{:S(2)}, u32[]{:S(2)}) collective-permute-start(f32[1,64]{1,0:T(1,128)S(1)} %get-tuple-element.299), channel_id=1, source_target_pairs={{28,0},{0,4},{4,8},{8,12},{12,16},{16,20},{20,24},{24,28},{29,1},{... | collective-permute-start | bytes 776 | tf_op jit(solution)/shard_map/while/body/eval_jaxpr/ppermute | solution.py:19
  118.6 6.4 %collective-permute-start.2 = (f32[1,64]{1,0:T(1,128)S(1)}, f32[1,64]{1,0:T(1,128)S(1)}, u32[]{:S(2)}, u32[]{:S(2)}) collective-permute-start(f32[1,64]{1,0:T(1,128)S(1)} %get-tuple-element.300), channel_id=1, source_target_pairs={{28,0},{0,4},{4,8},{8,12},{12,16},{16,20},{20,24},{24,28},{29,1},{... | collective-permute-start | bytes 776 | tf_op jit(solution)/shard_map/while/body/eval_jaxpr/ppermute | solution.py:19
  126.5 4.0 %copy-start.1 = (bf16[4096,576]{0,1:T(8,128)(2,1)S(1)}, bf16[4096,576]{0,1:T(8,128)(2,1)}, u32[]{:S(2)}) copy-start(bf16[4096,576]{0,1:T(8,128)(2,1)} %get-tuple-element.336) | copy-start | bytes 14155780 | tf_op jit(solution)/shard_map/while
  132.8 7.0 %collective-permute-start.3 = (f32[1,64,512]{2,1,0:T(8,128)S(1)}, f32[1,64,512]{2,1,0:T(8,128)}, u32[]{:S(2)}, u32[]{:S(2)}) collective-permute-start(f32[1,64,512]{2,1,0:T(8,128)S(1)} %fusion.112), channel_id=1, source_target_pairs={{28,0},{0,4},{4,8},{8,12},{12,16},{16,20},{20,24},{24,28},{29,1},{... | collective-permute-start | bytes 393224 | tf_op jit(solution)/shard_map/while/body/eval_jaxpr/ppermute | solution.py:19
  132.9 6.9 %collective-permute-start = (bf16[1,36864]{1,0:T(2,128)(2,1)S(1)}, bf16[1,36864]{1,0:T(2,128)(2,1)S(1)}, u32[]{:S(2)}, u32[]{:S(2)}) collective-permute-start(bf16[1,36864]{1,0:T(2,128)(2,1)S(1)} %copy.35), channel_id=1, source_target_pairs={{28,0},{0,4},{4,8},{8,12},{12,16},{16,20},{20,24},{24,28},{29,1},{... | collective-permute-start | bytes 221192 | tf_op jit(solution)/shard_map/while/body/eval_jaxpr/ppermute | solution.py:19
  133.0 6.8 %collective-permute-start.1 = (f32[1,64]{1,0:T(1,128)S(1)}, f32[1,64]{1,0:T(1,128)S(1)}, u32[]{:S(2)}, u32[]{:S(2)}) collective-permute-start(f32[1,64]{1,0:T(1,128)S(1)} %get-tuple-element.299), channel_id=1, source_target_pairs={{28,0},{0,4},{4,8},{8,12},{12,16},{16,20},{20,24},{24,28},{29,1},{... | collective-permute-start | bytes 776 | tf_op jit(solution)/shard_map/while/body/eval_jaxpr/ppermute | solution.py:19
  133.4 6.4 %collective-permute-start.2 = (f32[1,64]{1,0:T(1,128)S(1)}, f32[1,64]{1,0:T(1,128)S(1)}, u32[]{:S(2)}, u32[]{:S(2)}) collective-permute-start(f32[1,64]{1,0:T(1,128)S(1)} %get-tuple-element.300), channel_id=1, source_target_pairs={{28,0},{0,4},{4,8},{8,12},{12,16},{16,20},{20,24},{24,28},{29,1},{... | collective-permute-start | bytes 776 | tf_op jit(solution)/shard_map/while/body/eval_jaxpr/ppermute | solution.py:19
  139.8 9.8 %copy-start.4 = (s32[8]{0:T(128)S(1)}, s32[8]{0:T(128)}, u32[]{:S(2)}) copy-start(s32[8]{0:T(128)} %param.18) | copy-start | bytes 100
  139.9 15.2 %copy-start.5 = (bf16[4,1024,16]{1,2,0:T(8,128)(2,1)S(1)}, bf16[4,1024,16]{1,2,0:T(8,128)(2,1)}, u32[]{:S(2)}) copy-start(bf16[4,1024,16]{1,2,0:T(8,128)(2,1)} %param.28) | copy-start | bytes 393220
  139.9 15.4 %copy-start.2 = (bf16[4,16,7168]{2,1,0:T(8,128)(2,1)S(1)}, bf16[4,16,7168]{2,1,0:T(8,128)(2,1)}, u32[]{:S(2)}) copy-start(bf16[4,16,7168]{2,1,0:T(8,128)(2,1)} %param.29) | copy-start | bytes 2752516
  146.1 8.6 %all-to-all-start = ((bf16[8,2,2048]{2,1,0:T(2,128)(2,1)}), bf16[8,2,2048]{2,1,0:T(2,128)(2,1)S(1)}, u32[]{:S(2)}, u32[]{:S(2)}) async-start(bf16[8,2,2048]{2,1,0:T(2,128)(2,1)} %reshape.378), calls=%async_computation | async-start | bytes 131072 | tf_op jit(solution)/shard_map/all_to_all | solution.py:135
  149.6 66.1 %all-reduce.3.cloned.1.call-start = ((), (), s32[]{:S(2)}) async-start(), calls=%async_computation.1 | async-start | bytes 229376
  156.3 7.9 %copy-start.6 = (u32[32]{0:T(128)S(1)}, u32[32]{0:T(128)}, u32[]{:S(2)}) copy-start(u32[32]{0:T(128)} %constant.119) | copy-start | bytes 388
Sparse Core Ops, SparseCore 0:
  164.3 51.3 all-reduce.2
where the time goes:
time: 225 us
  waiting for transfers between devices  79.8 us (35%)
  matrix products  68.6 us (30%)
  starting transfers between devices  36.3 us (16%)
  other arithmetic  16.6 us (7%)
  between operations  13.6 us (6%)
  local copies, waits for them, and re-layouts  9.15 us (4%)
    unnamed x2, waiting for transfers between devices  51 us
    ppermute x32, starting transfers between devices, passed_along(): return lax.ppermute(block, axis, route)  32.7 us
    dot_general x8, matrix products, prefix_part(): jnp.einsum('nhk,tk->nht', queries, prefix_cache, preferred_element_type=j...  28.8 us
    ppermute x32, waiting for transfers between devices, passed_along(): return lax.ppermute(block, axis, route)  23.9 us
    dot_general x8, matrix products, partial_softmax(): jnp.einsum('nht,tl->nhl', weights_low, values, preferred_element_type=jnp...  18.5 us
    dot_general x1, matrix products, on_device(): jnp.dot(head_out, out_weight, preferred_element_type=jnp.float32)  7.84 us
    broadcast_in_dim x8, other arithmetic, prefix_part(): jnp.broadcast_to((mask_rows > 0)[:, :, None], (count_rows, blocks_here, B...  5.6 us
    all_to_all x1, waiting for transfers between devices, on_device(): lax.all_to_all(context, 'blk', split_axis=1, concat_axis=0, tiled=True)  4.95 us
  transfers between devices with their start and end apart: 34, of which 10 were waited for; matrix products, arithmetic and copies ran while one was open for 0% of the time, Pallas kernels for 0%

commit v1 on v0

--- a/solution.py
+++ b/solution.py
@@ -77,6 +77,15 @@
     adapter_oa,
     adapter_ob,
 ):
+
+    def tokens_plan(frame_in):
+        return jnp.concatenate(
+            lax.all_to_all(
+                jnp.stack(jnp.split(frame_in, lax.axis_size("blk"), 1), axis=0), "blk", 0, 0
+            ),
+            axis=0,
+        )
+
     score_scale = QK ** (-0.5)
     blk_count = lax.axis_size("blk")
     blk_index = lax.axis_index("blk")
@@ -132,7 +141,7 @@
     new_part = (new_scores, jnp.ones_like(new_scores), new_values)
     combined = combine_parts(combine_parts(prefix_result, suffix_result), new_part)
     context = (combined[2] / combined[1][..., None]).astype(jnp.bfloat16)
-    head_rows = lax.all_to_all(context, "blk", split_axis=1, concat_axis=0, tiled=True)
+    head_rows = tokens_plan(context)
     head_out = jnp.einsum("rhl,hlv->rhv", head_rows, value_up, preferred_element_type=jnp.float32)
     head_out = head_out.astype(jnp.bfloat16).reshape(group_rows, -1)
     group_hit = (tenant_ids[:, None] == jnp.arange(tenants)[None, :]).astype(jnp.float32)

time: 225 us -> 228 us (1.013)
  local copies, waits for them, and re-layouts: 9.15 us -> 12.6 us
    unnamed x18 -> x21, local copies, waits for them, and re-layouts: 3.96 us -> 6.87 us
where the time goes in v1:
time: 228 us; the launch traced here: 227 us
  waiting for transfers between devices  79.8 us (35%)
  matrix products  68.6 us (30%)
  starting transfers between devices  36.3 us (16%)
  other arithmetic  15.6 us (7%)
  between operations  13.5 us (6%)
  local copies, waits for them, and re-layouts  12.6 us (6%)
    unnamed x2, waiting for transfers between devices  51 us
    ppermute x32, starting transfers between devices, passed_along(): return lax.ppermute(block, axis, route)  32.7 us
    dot_general x8, matrix products, prefix_part(): jnp.einsum('nhk,tk->nht', queries, prefix_cache, preferred_element_type=j...  28.8 us
    ppermute x32, waiting for transfers between devices, passed_along(): return lax.ppermute(block, axis, route)  23.9 us
    dot_general x8, matrix products, partial_softmax(): jnp.einsum('nht,tl->nhl', weights_low, values, preferred_element_type=jnp...  18.5 us
    dot_general x1, matrix products, on_device(): jnp.dot(head_out, out_weight, preferred_element_type=jnp.float32)  7.84 us
    unnamed x21, local copies, waits for them, and re-layouts  6.87 us
    broadcast_in_dim x8, other arithmetic, prefix_part(): jnp.broadcast_to((mask_rows > 0)[:, :, None], (count_rows, blocks_here, B...  5.6 us
  transfers between devices with their start and end apart: 34, of which 10 were waited for; matrix products, arithmetic and copies ran while one was open for 0% of the time, Pallas kernels for 0%

profile of v1, /device:TPU:0, one launch (start us, length us, event | category | flops | bytes accessed | tf_op | source)
XLA Modules:
  0.0 227.1 jit_solution(130158430245078308)
XLA Ops:
  6.5 1.4 dynamic_slice.16
  7.9 0.7 compare_convert_fusion
  8.6 1.3 fusion.63
  10.2 0.7 slice_convert_fusion
  10.9 1.3 fusion.81
  12.2 0.7 iota_compare_fusion
  12.9 3.2 %fusion.80 = (bf16[36864]{0:T(1024)(128)(2,1)S(1)}, bf16[1,36864]{1,0:T(2,128)(2,1)S(1)}) fusion(bf16[64,1]{0,1:T(2,128)(2,1)S(1)} %reshape.367, bf16[64,36864]{1,0:T(8,128)(2,1)} %bitcast.208, bf16[1,36864]{1,0:T(2,128)(2,1)} %param.16), kind=kOutput, calls=%fused_computation.101 | convolution fusion | flops 4829184 | bytes 4939904 | tf_op jit(solution)/shard_map/dot_general | solution.py:105
  16.2 3.5 %fusion.82 = (f32[64]{0:T(128)S(1)}, f32[64,4096]{1,0:T(8,128)S(1)}) fusion(bf16[64,576]{1,0:T(8,128)(2,1)S(1)} %reshape.358, bf16[1,4096,576]{1,2,0:T(8,128)(2,1)} %param.23, pred[4096]{0:T(1024)(128)(4,1)S(1)} %iota_compare_fusion), kind=kOutput, calls=%fused_computation.103 | convolution fusion | flops 302776256 | bytes 5845248 | tf_op jit(solution)/shard_map/nhk,ntk->nht/dot_general | solution.py:129
  20.0 0.6 broadcast_in_dim.84
  20.7 119.1 %while.21 = (s32[]{:T(128)}, bf16[1,36864]{1,0:T(2,128)(2,1)S(1)}, f32[1,64]{1,0:T(1,128)S(1)}, f32[1,64]{1,0:T(1,128)S(1)}, f32[1,64,512]{2,1,0:T(8,128)}, /*in...) while((s32[]{:T(128)}, bf16[1,36864]{1,0:T(2,128)(2,1)S(1)}, ...), condition=%wide.region_4.5_spmd, body=%wide.region_1.4_spmd.sunk | while | flops 572359104 | bytes 32546200 | solution.py:123
  20.7 0.7 compare_bitcast_fusion.2
  22.2 3.6 %fusion.109 = (f32[64]{0:T(128)S(1)}, f32[64,4096]{1,0:T(8,128)S(1)}) fusion(bf16[64,576]{1,0:T(8,128)(2,1)S(1)} %reshape.380, bf16[4096,576]{0,1:T(8,128)(2,1)} %get-tuple-element.336, pred[4096]{0:T(1024)(128)(4,1)S(1)} %broadcast_bitcast_fusion.2), kind=kOutput, calls=%fused_computation.100.clone.1 | convolution fusion | flops 302776256 | bytes 5845248 | tf_op jit(solution)/shard_map/while/body/eval_jaxpr/nhk,tk->nht/dot_general | solution.py:48
  26.2 2.3 %fusion.112 = f32[1,64,512]{2,1,0:T(8,128)S(1)} fusion(bf16[4096,576]{0,1:T(8,128)(2,1)S(1)} %copy-done.1, f32[64,4096]{1,0:T(8,128)S(1)} %get-tuple-element.298, f32[64]{0:T(128)S(1)} %broadcast_maximum_fusion.3, f32[1,64,512]{2,1,0:T(8,128)} %get-tuple-element.320, f32[64]{0:T(128)S(1)} %get-tuple-element.301, f32[64]{0:T(128)S(1)} %get-tuple-element.302), kind=kOutput, calls=%fused_computation.6.clone.1 | convolution fusion | flops 269058048 | bytes 5506560 | tf_op jit(solution)/shard_map/while/body/eval_jaxpr/nht,tl->nhl/dot_general | solution.py:40
  29.0 2.6 %collective-permute-start = (bf16[1,36864]{1,0:T(2,128)(2,1)S(1)}, bf16[1,36864]{1,0:T(2,128)(2,1)S(1)}, u32[]{:S(2)}, u32[]{:S(2)}) collective-permute-start(bf16[1,36864]{1,0:T(2,128)(2,1)S(1)} %copy.27), channel_id=1, source_target_pairs={{28,0},{0,4},{4,8},{8,12},{12,16},{16,20},{20,24},{24,28},{29,1},{... | collective-permute-start | bytes 221192 | tf_op jit(solution)/shard_map/while/body/eval_jaxpr/ppermute | solution.py:19
  31.6 1.5 collective-permute-start.2
  33.2 3.0 %collective-permute-done.1 = f32[1,64]{1,0:T(1,128)S(1)} collective-permute-done((f32[1,64]{1,0:T(1,128)S(1)}, f32[1,64]{1,0:T(1,128)S(1)}, u32[]{:S(2)}, u32[]{:S(2)}) %collective-permute-start.1) | collective-permute-done | bytes 288 | tf_op jit(solution)/shard_map/while/body/eval_jaxpr/ppermute | solution.py:19
  36.2 0.7 compare_bitcast_fusion.2
  37.7 3.6 %fusion.109 = (f32[64]{0:T(128)S(1)}, f32[64,4096]{1,0:T(8,128)S(1)}) fusion(bf16[64,576]{1,0:T(8,128)(2,1)S(1)} %reshape.380, bf16[4096,576]{0,1:T(8,128)(2,1)} %get-tuple-element.336, pred[4096]{0:T(1024)(128)(4,1)S(1)} %broadcast_bitcast_fusion.2), kind=kOutput, calls=%fused_computation.100.clone.1 | convolution fusion | flops 302776256 | bytes 5845248 | tf_op jit(solution)/shard_map/while/body/eval_jaxpr/nhk,tk->nht/dot_general | solution.py:48
  41.7 2.3 %fusion.112 = f32[1,64,512]{2,1,0:T(8,128)S(1)} fusion(bf16[4096,576]{0,1:T(8,128)(2,1)S(1)} %copy-done.1, f32[64,4096]{1,0:T(8,128)S(1)} %get-tuple-element.298, f32[64]{0:T(128)S(1)} %broadcast_maximum_fusion.3, f32[1,64,512]{2,1,0:T(8,128)} %get-tuple-element.320, f32[64]{0:T(128)S(1)} %get-tuple-element.301, f32[64]{0:T(128)S(1)} %get-tuple-element.302), kind=kOutput, calls=%fused_computation.6.clone.1 | convolution fusion | flops 269058048 | bytes 5506560 | tf_op jit(solution)/shard_map/while/body/eval_jaxpr/nht,tl->nhl/dot_general | solution.py:40
  44.1 1.4 collective-permute-start
  45.6 2.4 %collective-permute-start.2 = (f32[1,64]{1,0:T(1,128)S(1)}, f32[1,64]{1,0:T(1,128)S(1)}, u32[]{:S(2)}, u32[]{:S(2)}) collective-permute-start(f32[1,64]{1,0:T(1,128)S(1)} %get-tuple-element.300), channel_id=1, source_target_pairs={{28,0},{0,4},{4,8},{8,12},{12,16},{16,20},{20,24},{24,28},{29,1},{... | collective-permute-start | bytes 776 | tf_op jit(solution)/shard_map/while/body/eval_jaxpr/ppermute | solution.py:19
  48.0 3.0 %collective-permute-done.1 = f32[1,64]{1,0:T(1,128)S(1)} collective-permute-done((f32[1,64]{1,0:T(1,128)S(1)}, f32[1,64]{1,0:T(1,128)S(1)}, u32[]{:S(2)}, u32[]{:S(2)}) %collective-permute-start.1) | collective-permute-done | bytes 288 | tf_op jit(solution)/shard_map/while/body/eval_jaxpr/ppermute | solution.py:19
  51.0 0.7 compare_bitcast_fusion.2
  52.5 3.6 %fusion.109 = (f32[64]{0:T(128)S(1)}, f32[64,4096]{1,0:T(8,128)S(1)}) fusion(bf16[64,576]{1,0:T(8,128)(2,1)S(1)} %reshape.380, bf16[4096,576]{0,1:T(8,128)(2,1)} %get-tuple-element.336, pred[4096]{0:T(1024)(128)(4,1)S(1)} %broadcast_bitcast_fusion.2), kind=kOutput, calls=%fused_computation.100.clone.1 | convolution fusion | flops 302776256 | bytes 5845248 | tf_op jit(solution)/shard_map/while/body/eval_jaxpr/nhk,tk->nht/dot_general | solution.py:48
  56.5 2.3 %fusion.112 = f32[1,64,512]{2,1,0:T(8,128)S(1)} fusion(bf16[4096,576]{0,1:T(8,128)(2,1)S(1)} %copy-done.1, f32[64,4096]{1,0:T(8,128)S(1)} %get-tuple-element.298, f32[64]{0:T(128)S(1)} %broadcast_maximum_fusion.3, f32[1,64,512]{2,1,0:T(8,128)} %get-tuple-element.320, f32[64]{0:T(128)S(1)} %get-tuple-element.301, f32[64]{0:T(128)S(1)} %get-tuple-element.302), kind=kOutput, calls=%fused_computation.6.clone.1 | convolution fusion | flops 269058048 | bytes 5506560 | tf_op jit(solution)/shard_map/while/body/eval_jaxpr/nht,tl->nhl/dot_general | solution.py:40
  59.5 3.3 %collective-permute-start.2 = (f32[1,64]{1,0:T(1,128)S(1)}, f32[1,64]{1,0:T(1,128)S(1)}, u32[]{:S(2)}, u32[]{:S(2)}) collective-permute-start(f32[1,64]{1,0:T(1,128)S(1)} %get-tuple-element.300), channel_id=1, source_target_pairs={{28,0},{0,4},{4,8},{8,12},{12,16},{16,20},{20,24},{24,28},{29,1},{... | collective-permute-start | bytes 776 | tf_op jit(solution)/shard_map/while/body/eval_jaxpr/ppermute | solution.py:19
  62.8 3.0 %collective-permute-done.1 = f32[1,64]{1,0:T(1,128)S(1)} collective-permute-done((f32[1,64]{1,0:T(1,128)S(1)}, f32[1,64]{1,0:T(1,128)S(1)}, u32[]{:S(2)}, u32[]{:S(2)}) %collective-permute-start.1) | collective-permute-done | bytes 288 | tf_op jit(solution)/shard_map/while/body/eval_jaxpr/ppermute | solution.py:19
  65.8 0.7 compare_bitcast_fusion.2
  67.3 3.6 %fusion.109 = (f32[64]{0:T(128)S(1)}, f32[64,4096]{1,0:T(8,128)S(1)}) fusion(bf16[64,576]{1,0:T(8,128)(2,1)S(1)} %reshape.380, bf16[4096,576]{0,1:T(8,128)(2,1)} %get-tuple-element.336, pred[4096]{0:T(1024)(128)(4,1)S(1)} %broadcast_bitcast_fusion.2), kind=kOutput, calls=%fused_computation.100.clone.1 | convolution fusion | flops 302776256 | bytes 5845248 | tf_op jit(solution)/shard_map/while/body/eval_jaxpr/nhk,tk->nht/dot_general | solution.py:48
  71.3 2.3 %fusion.112 = f32[1,64,512]{2,1,0:T(8,128)S(1)} fusion(bf16[4096,576]{0,1:T(8,128)(2,1)S(1)} %copy-done.1, f32[64,4096]{1,0:T(8,128)S(1)} %get-tuple-element.298, f32[64]{0:T(128)S(1)} %broadcast_maximum_fusion.3, f32[1,64,512]{2,1,0:T(8,128)} %get-tuple-element.320, f32[64]{0:T(128)S(1)} %get-tuple-element.301, f32[64]{0:T(128)S(1)} %get-tuple-element.302), kind=kOutput, calls=%fused_computation.6.clone.1 | convolution fusion | flops 269058048 | bytes 5506560 | tf_op jit(solution)/shard_map/while/body/eval_jaxpr/nht,tl->nhl/dot_general | solution.py:40
  74.2 3.4 %collective-permute-start.2 = (f32[1,64]{1,0:T(1,128)S(1)}, f32[1,64]{1,0:T(1,128)S(1)}, u32[]{:S(2)}, u32[]{:S(2)}) collective-permute-start(f32[1,64]{1,0:T(1,128)S(1)} %get-tuple-element.300), channel_id=1, source_target_pairs={{28,0},{0,4},{4,8},{8,12},{12,16},{16,20},{20,24},{24,28},{29,1},{... | collective-permute-start | bytes 776 | tf_op jit(solution)/shard_map/while/body/eval_jaxpr/ppermute | solution.py:19
  77.6 3.0 %collective-permute-done.1 = f32[1,64]{1,0:T(1,128)S(1)} collective-permute-done((f32[1,64]{1,0:T(1,128)S(1)}, f32[1,64]{1,0:T(1,128)S(1)}, u32[]{:S(2)}, u32[]{:S(2)}) %collective-permute-start.1) | collective-permute-done | bytes 288 | tf_op jit(solution)/shard_map/while/body/eval_jaxpr/ppermute | solution.py:19
  80.6 0.7 compare_bitcast_fusion.2
  82.1 3.6 %fusion.109 = (f32[64]{0:T(128)S(1)}, f32[64,4096]{1,0:T(8,128)S(1)}) fusion(bf16[64,576]{1,0:T(8,128)(2,1)S(1)} %reshape.380, bf16[4096,576]{0,1:T(8,128)(2,1)} %get-tuple-element.336, pred[4096]{0:T(1024)(128)(4,1)S(1)} %broadcast_bitcast_fusion.2), kind=kOutput, calls=%fused_computation.100.clone.1 | convolution fusion | flops 302776256 | bytes 5845248 | tf_op jit(solution)/shard_map/while/body/eval_jaxpr/nhk,tk->nht/dot_general | solution.py:48
  86.1 2.3 %fusion.112 = f32[1,64,512]{2,1,0:T(8,128)S(1)} fusion(bf16[4096,576]{0,1:T(8,128)(2,1)S(1)} %copy-done.1, f32[64,4096]{1,0:T(8,128)S(1)} %get-tuple-element.298, f32[64]{0:T(128)S(1)} %broadcast_maximum_fusion.3, f32[1,64,512]{2,1,0:T(8,128)} %get-tuple-element.320, f32[64]{0:T(128)S(1)} %get-tuple-element.301, f32[64]{0:T(128)S(1)} %get-tuple-element.302), kind=kOutput, calls=%fused_computation.6.clone.1 | convolution fusion | flops 269058048 | bytes 5506560 | tf_op jit(solution)/shard_map/while/body/eval_jaxpr/nht,tl->nhl/dot_general | solution.py:40
  89.0 3.4 %collective-permute-start.2 = (f32[1,64]{1,0:T(1,128)S(1)}, f32[1,64]{1,0:T(1,128)S(1)}, u32[]{:S(2)}, u32[]{:S(2)}) collective-permute-start(f32[1,64]{1,0:T(1,128)S(1)} %get-tuple-element.300), channel_id=1, source_target_pairs={{28,0},{0,4},{4,8},{8,12},{12,16},{16,20},{20,24},{24,28},{29,1},{... | collective-permute-start | bytes 776 | tf_op jit(solution)/shard_map/while/body/eval_jaxpr/ppermute | solution.py:19
  92.4 3.0 %collective-permute-done.1 = f32[1,64]{1,0:T(1,128)S(1)} collective-permute-done((f32[1,64]{1,0:T(1,128)S(1)}, f32[1,64]{1,0:T(1,128)S(1)}, u32[]{:S(2)}, u32[]{:S(2)}) %collective-permute-start.1) | collective-permute-done | bytes 288 | tf_op jit(solution)/shard_map/while/body/eval_jaxpr/ppermute | solution.py:19
  95.4 0.7 compare_bitcast_fusion.2
  96.9 3.6 %fusion.109 = (f32[64]{0:T(128)S(1)}, f32[64,4096]{1,0:T(8,128)S(1)}) fusion(bf16[64,576]{1,0:T(8,128)(2,1)S(1)} %reshape.380, bf16[4096,576]{0,1:T(8,128)(2,1)} %get-tuple-element.336, pred[4096]{0:T(1024)(128)(4,1)S(1)} %broadcast_bitcast_fusion.2), kind=kOutput, calls=%fused_computation.100.clone.1 | convolution fusion | flops 302776256 | bytes 5845248 | tf_op jit(solution)/shard_map/while/body/eval_jaxpr/nhk,tk->nht/dot_general | solution.py:48
  100.9 2.3 %fusion.112 = f32[1,64,512]{2,1,0:T(8,128)S(1)} fusion(bf16[4096,576]{0,1:T(8,128)(2,1)S(1)} %copy-done.1, f32[64,4096]{1,0:T(8,128)S(1)} %get-tuple-element.298, f32[64]{0:T(128)S(1)} %broadcast_maximum_fusion.3, f32[1,64,512]{2,1,0:T(8,128)} %get-tuple-element.320, f32[64]{0:T(128)S(1)} %get-tuple-element.301, f32[64]{0:T(128)S(1)} %get-tuple-element.302), kind=kOutput, calls=%fused_computation.6.clone.1 | convolution fusion | flops 269058048 | bytes 5506560 | tf_op jit(solution)/shard_map/while/body/eval_jaxpr/nht,tl->nhl/dot_general | solution.py:40
  103.8 3.4 %collective-permute-start.2 = (f32[1,64]{1,0:T(1,128)S(1)}, f32[1,64]{1,0:T(1,128)S(1)}, u32[]{:S(2)}, u32[]{:S(2)}) collective-permute-start(f32[1,64]{1,0:T(1,128)S(1)} %get-tuple-element.300), channel_id=1, source_target_pairs={{28,0},{0,4},{4,8},{8,12},{12,16},{16,20},{20,24},{24,28},{29,1},{... | collective-permute-start | bytes 776 | tf_op jit(solution)/shard_map/while/body/eval_jaxpr/ppermute | solution.py:19
  107.2 3.0 %collective-permute-done.1 = f32[1,64]{1,0:T(1,128)S(1)} collective-permute-done((f32[1,64]{1,0:T(1,128)S(1)}, f32[1,64]{1,0:T(1,128)S(1)}, u32[]{:S(2)}, u32[]{:S(2)}) %collective-permute-start.1) | collective-permute-done | bytes 288 | tf_op jit(solution)/shard_map/while/body/eval_jaxpr/ppermute | solution.py:19
  110.3 0.7 compare_bitcast_fusion.2
  111.7 3.6 %fusion.109 = (f32[64]{0:T(128)S(1)}, f32[64,4096]{1,0:T(8,128)S(1)}) fusion(bf16[64,576]{1,0:T(8,128)(2,1)S(1)} %reshape.380, bf16[4096,576]{0,1:T(8,128)(2,1)} %get-tuple-element.336, pred[4096]{0:T(1024)(128)(4,1)S(1)} %broadcast_bitcast_fusion.2), kind=kOutput, calls=%fused_computation.100.clone.1 | convolution fusion | flops 302776256 | bytes 5845248 | tf_op jit(solution)/shard_map/while/body/eval_jaxpr/nhk,tk->nht/dot_general | solution.py:48
  115.7 2.3 %fusion.112 = f32[1,64,512]{2,1,0:T(8,128)S(1)} fusion(bf16[4096,576]{0,1:T(8,128)(2,1)S(1)} %copy-done.1, f32[64,4096]{1,0:T(8,128)S(1)} %get-tuple-element.298, f32[64]{0:T(128)S(1)} %broadcast_maximum_fusion.3, f32[1,64,512]{2,1,0:T(8,128)} %get-tuple-element.320, f32[64]{0:T(128)S(1)} %get-tuple-element.301, f32[64]{0:T(128)S(1)} %get-tuple-element.302), kind=kOutput, calls=%fused_computation.6.clone.1 | convolution fusion | flops 269058048 | bytes 5506560 | tf_op jit(solution)/shard_map/while/body/eval_jaxpr/nht,tl->nhl/dot_general | solution.py:40
  118.6 3.4 %collective-permute-start.2 = (f32[1,64]{1,0:T(1,128)S(1)}, f32[1,64]{1,0:T(1,128)S(1)}, u32[]{:S(2)}, u32[]{:S(2)}) collective-permute-start(f32[1,64]{1,0:T(1,128)S(1)} %get-tuple-element.300), channel_id=1, source_target_pairs={{28,0},{0,4},{4,8},{8,12},{12,16},{16,20},{20,24},{24,28},{29,1},{... | collective-permute-start | bytes 776 | tf_op jit(solution)/shard_map/while/body/eval_jaxpr/ppermute | solution.py:19
  122.0 3.0 %collective-permute-done.1 = f32[1,64]{1,0:T(1,128)S(1)} collective-permute-done((f32[1,64]{1,0:T(1,128)S(1)}, f32[1,64]{1,0:T(1,128)S(1)}, u32[]{:S(2)}, u32[]{:S(2)}) %collective-permute-start.1) | collective-permute-done | bytes 288 | tf_op jit(solution)/shard_map/while/body/eval_jaxpr/ppermute | solution.py:19
  125.1 0.7 compare_bitcast_fusion.2
  126.5 3.6 %fusion.109 = (f32[64]{0:T(128)S(1)}, f32[64,4096]{1,0:T(8,128)S(1)}) fusion(bf16[64,576]{1,0:T(8,128)(2,1)S(1)} %reshape.380, bf16[4096,576]{0,1:T(8,128)(2,1)} %get-tuple-element.336, pred[4096]{0:T(1024)(128)(4,1)S(1)} %broadcast_bitcast_fusion.2), kind=kOutput, calls=%fused_computation.100.clone.1 | convolution fusion | flops 302776256 | bytes 5845248 | tf_op jit(solution)/shard_map/while/body/eval_jaxpr/nhk,tk->nht/dot_general | solution.py:48
  130.5 2.3 %fusion.112 = f32[1,64,512]{2,1,0:T(8,128)S(1)} fusion(bf16[4096,576]{0,1:T(8,128)(2,1)S(1)} %copy-done.1, f32[64,4096]{1,0:T(8,128)S(1)} %get-tuple-element.298, f32[64]{0:T(128)S(1)} %broadcast_maximum_fusion.3, f32[1,64,512]{2,1,0:T(8,128)} %get-tuple-element.320, f32[64]{0:T(128)S(1)} %get-tuple-element.301, f32[64]{0:T(128)S(1)} %get-tuple-element.302), kind=kOutput, calls=%fused_computation.6.clone.1 | convolution fusion | flops 269058048 | bytes 5506560 | tf_op jit(solution)/shard_map/while/body/eval_jaxpr/nht,tl->nhl/dot_general | solution.py:40
  133.4 3.4 %collective-permute-start.2 = (f32[1,64]{1,0:T(1,128)S(1)}, f32[1,64]{1,0:T(1,128)S(1)}, u32[]{:S(2)}, u32[]{:S(2)}) collective-permute-start(f32[1,64]{1,0:T(1,128)S(1)} %get-tuple-element.300), channel_id=1, source_target_pairs={{28,0},{0,4},{4,8},{8,12},{12,16},{16,20},{20,24},{24,28},{29,1},{... | collective-permute-start | bytes 776 | tf_op jit(solution)/shard_map/while/body/eval_jaxpr/ppermute | solution.py:19
  136.8 3.0 %collective-permute-done.1 = f32[1,64]{1,0:T(1,128)S(1)} collective-permute-done((f32[1,64]{1,0:T(1,128)S(1)}, f32[1,64]{1,0:T(1,128)S(1)}, u32[]{:S(2)}, u32[]{:S(2)}) %collective-permute-start.1) | collective-permute-done | bytes 288 | tf_op jit(solution)/shard_map/while/body/eval_jaxpr/ppermute | solution.py:19
  140.0 3.8 %fusion.53 = bf16[1,64,512]{2,1,0:T(8,128)(2,1)S(1)} fusion(bf16[1,4096,576]{1,2,0:T(8,128)(2,1)} %param.23, f32[64,4096]{1,0:T(8,128)S(1)} %get-tuple-element.239, f32[64]{0:T(128)S(1)} %broadcast_maximum_fusion.1, f32[1,64,512]{2,1,0:T(8,128)} %get-tuple-element.206, f32[64]{0:T(128)S(1)} %get-tuple-element.232, f32[64]{0:T(128)S(1)} %get-tuple-element.233, ...), kind=kOutput, calls=%fused_computation.45 | convolution fusion | flops 269221888 | bytes 5443072 | tf_op jit(solution)/shard_map/nht,ntl->nhl/dot_general | solution.py:38
  143.8 0.6 constant_dynamic-update-slice_fusion.7
  145.6 0.6 constant_dynamic-update-slice_fusion.4
  146.8 0.6 constant_dynamic-update-slice_fusion.2
  147.4 0.6 constant_dynamic-update-slice_fusion.1
  148.0 0.6 constant_dynamic-update-slice_fusion
  148.6 3.5 %all-to-all-start = ((bf16[8,1,8,512]{3,2,1,0:T(8,128)(2,1)}), bf16[8,1,8,512]{3,2,1,0:T(8,128)(2,1)S(1)}, u32[]{:S(2)}, u32[]{:S(2)}) async-start(bf16[8,1,8,512]{3,2,1,0:T(8,128)(2,1)} %constant_dynamic-update-slice_fusion), calls=%async_computation | async-start | bytes 131072 | tf_op jit(solution)/shard_map/all_to_all | solution.py:83
  152.2 5.0 %all-to-all-done = bf16[8,1,8,512]{3,2,1,0:T(8,128)(2,1)S(1)} async-done(((bf16[8,1,8,512]{3,2,1,0:T(8,128)(2,1)}), bf16[8,1,8,512]{3,2,1,0:T(8,128)(2,1)S(1)}, u32[]{:S(2)}, u32[]{:S(2)}) %all-to-all-start) | async-done | bytes 65568 | tf_op jit(solution)/shard_map/all_to_all | solution.py:83
  157.6 1.1 convolution_bitcast_fusion
  158.7 7.8 %fusion.21 = bf16[8,7168]{1,0:T(8,128)(2,1)} fusion(f32[8,7168]{1,0:T(8,128)S(1)} %convolution_bitcast_fusion, bf16[1024,7168]{1,0:T(8,128)(2,1)} %param.27, bf16[8,8,128]{2,1,0:T(8,128)(2,1)S(1)} %convolution_convert_fusion), kind=kOutput, calls=%fused_computation.26 | convolution fusion | flops 117555200 | bytes 15040512 | tf_op jit(solution)/shard_map/dot_general | solution.py:149
  167.2 50.9 %all-reduce.3.cloned.1.call-done = bf16[8,7168]{1,0:T(8,128)(2,1)} async-done(((bf16[8,7168]{1,0:T(8,128)(2,1)}), bf16[8,7168]{1,0:T(8,128)(2,1)}) %all-reduce.3.cloned.1.call-update) | async-done | bytes 114704
  218.1 2.1 constant_dynamic-slice_fusion
  (148 shorter events, 17.1 us)
Async XLA Ops:
  6.5 150.6 %copy-start = (bf16[8,512,128]{2,1,0:T(8,128)(2,1)S(1)}, bf16[8,512,128]{2,1,0:T(8,128)(2,1)}, u32[]{:S(2)}) copy-start(bf16[8,512,128]{2,1,0:T(8,128)(2,1)} %param.26) | copy-start | bytes 3145732
  20.7 119.2 %copy-start.3 = (bf16[1,576]{1,0:T(2,128)(2,1)S(1)}, bf16[1,576]{1,0:T(2,128)(2,1)}, u32[]{:S(2)}) copy-start(bf16[1,576]{1,0:T(2,128)(2,1)} %param.25) | copy-start | bytes 3460
  22.2 4.0 %copy-start.1 = (bf16[4096,576]{0,1:T(8,128)(2,1)S(1)}, bf16[4096,576]{0,1:T(8,128)(2,1)}, u32[]{:S(2)}) copy-start(bf16[4096,576]{0,1:T(8,128)(2,1)} %get-tuple-element.336) | copy-start | bytes 14155780 | tf_op jit(solution)/shard_map/while
  28.5 7.7 %collective-permute-start.3 = (f32[1,64,512]{2,1,0:T(8,128)S(1)}, f32[1,64,512]{2,1,0:T(8,128)}, u32[]{:S(2)}, u32[]{:S(2)}) collective-permute-start(f32[1,64,512]{2,1,0:T(8,128)S(1)} %fusion.112), channel_id=1, source_target_pairs={{28,0},{0,4},{4,8},{8,12},{12,16},{16,20},{20,24},{24,28},{29,1},{... | collective-permute-start | bytes 393224 | tf_op jit(solution)/shard_map/while/body/eval_jaxpr/ppermute | solution.py:19
  29.0 7.2 %collective-permute-start = (bf16[1,36864]{1,0:T(2,128)(2,1)S(1)}, bf16[1,36864]{1,0:T(2,128)(2,1)S(1)}, u32[]{:S(2)}, u32[]{:S(2)}) collective-permute-start(bf16[1,36864]{1,0:T(2,128)(2,1)S(1)} %copy.27), channel_id=1, source_target_pairs={{28,0},{0,4},{4,8},{8,12},{12,16},{16,20},{20,24},{24,28},{29,1},{... | collective-permute-start | bytes 221192 | tf_op jit(solution)/shard_map/while/body/eval_jaxpr/ppermute | solution.py:19
  31.6 4.6 %collective-permute-start.1 = (f32[1,64]{1,0:T(1,128)S(1)}, f32[1,64]{1,0:T(1,128)S(1)}, u32[]{:S(2)}, u32[]{:S(2)}) collective-permute-start(f32[1,64]{1,0:T(1,128)S(1)} %get-tuple-element.299), channel_id=1, source_target_pairs={{28,0},{0,4},{4,8},{8,12},{12,16},{16,20},{20,24},{24,28},{29,1},{... | collective-permute-start | bytes 776 | tf_op jit(solution)/shard_map/while/body/eval_jaxpr/ppermute | solution.py:19
  31.6 4.5 %collective-permute-start.2 = (f32[1,64]{1,0:T(1,128)S(1)}, f32[1,64]{1,0:T(1,128)S(1)}, u32[]{:S(2)}, u32[]{:S(2)}) collective-permute-start(f32[1,64]{1,0:T(1,128)S(1)} %get-tuple-element.300), channel_id=1, source_target_pairs={{28,0},{0,4},{4,8},{8,12},{12,16},{16,20},{20,24},{24,28},{29,1},{... | collective-permute-start | bytes 776 | tf_op jit(solution)/shard_map/while/body/eval_jaxpr/ppermute | solution.py:19
  37.7 4.0 %copy-start.1 = (bf16[4096,576]{0,1:T(8,128)(2,1)S(1)}, bf16[4096,576]{0,1:T(8,128)(2,1)}, u32[]{:S(2)}) copy-start(bf16[4096,576]{0,1:T(8,128)(2,1)} %get-tuple-element.336) | copy-start | bytes 14155780 | tf_op jit(solution)/shard_map/while
  44.0 7.0 %collective-permute-start.3 = (f32[1,64,512]{2,1,0:T(8,128)S(1)}, f32[1,64,512]{2,1,0:T(8,128)}, u32[]{:S(2)}, u32[]{:S(2)}) collective-permute-start(f32[1,64,512]{2,1,0:T(8,128)S(1)} %fusion.112), channel_id=1, source_target_pairs={{28,0},{0,4},{4,8},{8,12},{12,16},{16,20},{20,24},{24,28},{29,1},{... | collective-permute-start | bytes 393224 | tf_op jit(solution)/shard_map/while/body/eval_jaxpr/ppermute | solution.py:19
  44.1 6.9 %collective-permute-start = (bf16[1,36864]{1,0:T(2,128)(2,1)S(1)}, bf16[1,36864]{1,0:T(2,128)(2,1)S(1)}, u32[]{:S(2)}, u32[]{:S(2)}) collective-permute-start(bf16[1,36864]{1,0:T(2,128)(2,1)S(1)} %copy.27), channel_id=1, source_target_pairs={{28,0},{0,4},{4,8},{8,12},{12,16},{16,20},{20,24},{24,28},{29,1},{... | collective-permute-start | bytes 221192 | tf_op jit(solution)/shard_map/while/body/eval_jaxpr/ppermute | solution.py:19
  45.5 5.5 %collective-permute-start.1 = (f32[1,64]{1,0:T(1,128)S(1)}, f32[1,64]{1,0:T(1,128)S(1)}, u32[]{:S(2)}, u32[]{:S(2)}) collective-permute-start(f32[1,64]{1,0:T(1,128)S(1)} %get-tuple-element.299), channel_id=1, source_target_pairs={{28,0},{0,4},{4,8},{8,12},{12,16},{16,20},{20,24},{24,28},{29,1},{... | collective-permute-start | bytes 776 | tf_op jit(solution)/shard_map/while/body/eval_jaxpr/ppermute | solution.py:19
  45.6 5.4 %collective-permute-start.2 = (f32[1,64]{1,0:T(1,128)S(1)}, f32[1,64]{1,0:T(1,128)S(1)}, u32[]{:S(2)}, u32[]{:S(2)}) collective-permute-start(f32[1,64]{1,0:T(1,128)S(1)} %get-tuple-element.300), channel_id=1, source_target_pairs={{28,0},{0,4},{4,8},{8,12},{12,16},{16,20},{20,24},{24,28},{29,1},{... | collective-permute-start | bytes 776 | tf_op jit(solution)/shard_map/while/body/eval_jaxpr/ppermute | solution.py:19
  52.5 4.0 %copy-start.1 = (bf16[4096,576]{0,1:T(8,128)(2,1)S(1)}, bf16[4096,576]{0,1:T(8,128)(2,1)}, u32[]{:S(2)}) copy-start(bf16[4096,576]{0,1:T(8,128)(2,1)} %get-tuple-element.336) | copy-start | bytes 14155780 | tf_op jit(solution)/shard_map/while
  58.8 7.0 %collective-permute-start.3 = (f32[1,64,512]{2,1,0:T(8,128)S(1)}, f32[1,64,512]{2,1,0:T(8,128)}, u32[]{:S(2)}, u32[]{:S(2)}) collective-permute-start(f32[1,64,512]{2,1,0:T(8,128)S(1)} %fusion.112), channel_id=1, source_target_pairs={{28,0},{0,4},{4,8},{8,12},{12,16},{16,20},{20,24},{24,28},{29,1},{... | collective-permute-start | bytes 393224 | tf_op jit(solution)/shard_map/while/body/eval_jaxpr/ppermute | solution.py:19
  58.9 6.9 %collective-permute-start = (bf16[1,36864]{1,0:T(2,128)(2,1)S(1)}, bf16[1,36864]{1,0:T(2,128)(2,1)S(1)}, u32[]{:S(2)}, u32[]{:S(2)}) collective-permute-start(bf16[1,36864]{1,0:T(2,128)(2,1)S(1)} %copy.27), channel_id=1, source_target_pairs={{28,0},{0,4},{4,8},{8,12},{12,16},{16,20},{20,24},{24,28},{29,1},{... | collective-permute-start | bytes 221192 | tf_op jit(solution)/shard_map/while/body/eval_jaxpr/ppermute | solution.py:19
  59.4 6.4 %collective-permute-start.1 = (f32[1,64]{1,0:T(1,128)S(1)}, f32[1,64]{1,0:T(1,128)S(1)}, u32[]{:S(2)}, u32[]{:S(2)}) collective-permute-start(f32[1,64]{1,0:T(1,128)S(1)} %get-tuple-element.299), channel_id=1, source_target_pairs={{28,0},{0,4},{4,8},{8,12},{12,16},{16,20},{20,24},{24,28},{29,1},{... | collective-permute-start | bytes 776 | tf_op jit(solution)/shard_map/while/body/eval_jaxpr/ppermute | solution.py:19
  59.5 6.3 %collective-permute-start.2 = (f32[1,64]{1,0:T(1,128)S(1)}, f32[1,64]{1,0:T(1,128)S(1)}, u32[]{:S(2)}, u32[]{:S(2)}) collective-permute-start(f32[1,64]{1,0:T(1,128)S(1)} %get-tuple-element.300), channel_id=1, source_target_pairs={{28,0},{0,4},{4,8},{8,12},{12,16},{16,20},{20,24},{24,28},{29,1},{... | collective-permute-start | bytes 776 | tf_op jit(solution)/shard_map/while/body/eval_jaxpr/ppermute | solution.py:19
  67.3 4.0 %copy-start.1 = (bf16[4096,576]{0,1:T(8,128)(2,1)S(1)}, bf16[4096,576]{0,1:T(8,128)(2,1)}, u32[]{:S(2)}) copy-start(bf16[4096,576]{0,1:T(8,128)(2,1)} %get-tuple-element.336) | copy-start | bytes 14155780 | tf_op jit(solution)/shard_map/while
  73.6 7.0 %collective-permute-start.3 = (f32[1,64,512]{2,1,0:T(8,128)S(1)}, f32[1,64,512]{2,1,0:T(8,128)}, u32[]{:S(2)}, u32[]{:S(2)}) collective-permute-start(f32[1,64,512]{2,1,0:T(8,128)S(1)} %fusion.112), channel_id=1, source_target_pairs={{28,0},{0,4},{4,8},{8,12},{12,16},{16,20},{20,24},{24,28},{29,1},{... | collective-permute-start | bytes 393224 | tf_op jit(solution)/shard_map/while/body/eval_jaxpr/ppermute | solution.py:19
  73.7 6.9 %collective-permute-start = (bf16[1,36864]{1,0:T(2,128)(2,1)S(1)}, bf16[1,36864]{1,0:T(2,128)(2,1)S(1)}, u32[]{:S(2)}, u32[]{:S(2)}) collective-permute-start(bf16[1,36864]{1,0:T(2,128)(2,1)S(1)} %copy.27), channel_id=1, source_target_pairs={{28,0},{0,4},{4,8},{8,12},{12,16},{16,20},{20,24},{24,28},{29,1},{... | collective-permute-start | bytes 221192 | tf_op jit(solution)/shard_map/while/body/eval_jaxpr/ppermute | solution.py:19
  73.7 6.8 %collective-permute-start.1 = (f32[1,64]{1,0:T(1,128)S(1)}, f32[1,64]{1,0:T(1,128)S(1)}, u32[]{:S(2)}, u32[]{:S(2)}) collective-permute-start(f32[1,64]{1,0:T(1,128)S(1)} %get-tuple-element.299), channel_id=1, source_target_pairs={{28,0},{0,4},{4,8},{8,12},{12,16},{16,20},{20,24},{24,28},{29,1},{... | collective-permute-start | bytes 776 | tf_op jit(solution)/shard_map/while/body/eval_jaxpr/ppermute | solution.py:19
  74.2 6.4 %collective-permute-start.2 = (f32[1,64]{1,0:T(1,128)S(1)}, f32[1,64]{1,0:T(1,128)S(1)}, u32[]{:S(2)}, u32[]{:S(2)}) collective-permute-start(f32[1,64]{1,0:T(1,128)S(1)} %get-tuple-element.300), channel_id=1, source_target_pairs={{28,0},{0,4},{4,8},{8,12},{12,16},{16,20},{20,24},{24,28},{29,1},{... | collective-permute-start | bytes 776 | tf_op jit(solution)/shard_map/while/body/eval_jaxpr/ppermute | solution.py:19
  82.1 4.0 %copy-start.1 = (bf16[4096,576]{0,1:T(8,128)(2,1)S(1)}, bf16[4096,576]{0,1:T(8,128)(2,1)}, u32[]{:S(2)}) copy-start(bf16[4096,576]{0,1:T(8,128)(2,1)} %get-tuple-element.336) | copy-start | bytes 14155780 | tf_op jit(solution)/shard_map/while
  88.4 7.0 %collective-permute-start.3 = (f32[1,64,512]{2,1,0:T(8,128)S(1)}, f32[1,64,512]{2,1,0:T(8,128)}, u32[]{:S(2)}, u32[]{:S(2)}) collective-permute-start(f32[1,64,512]{2,1,0:T(8,128)S(1)} %fusion.112), channel_id=1, source_target_pairs={{28,0},{0,4},{4,8},{8,12},{12,16},{16,20},{20,24},{24,28},{29,1},{... | collective-permute-start | bytes 393224 | tf_op jit(solution)/shard_map/while/body/eval_jaxpr/ppermute | solution.py:19
  88.5 6.9 %collective-permute-start = (bf16[1,36864]{1,0:T(2,128)(2,1)S(1)}, bf16[1,36864]{1,0:T(2,128)(2,1)S(1)}, u32[]{:S(2)}, u32[]{:S(2)}) collective-permute-start(bf16[1,36864]{1,0:T(2,128)(2,1)S(1)} %copy.27), channel_id=1, source_target_pairs={{28,0},{0,4},{4,8},{8,12},{12,16},{16,20},{20,24},{24,28},{29,1},{... | collective-permute-start | bytes 221192 | tf_op jit(solution)/shard_map/while/body/eval_jaxpr/ppermute | solution.py:19
  88.6 6.8 %collective-permute-start.1 = (f32[1,64]{1,0:T(1,128)S(1)}, f32[1,64]{1,0:T(1,128)S(1)}, u32[]{:S(2)}, u32[]{:S(2)}) collective-permute-start(f32[1,64]{1,0:T(1,128)S(1)} %get-tuple-element.299), channel_id=1, source_target_pairs={{28,0},{0,4},{4,8},{8,12},{12,16},{16,20},{20,24},{24,28},{29,1},{... | collective-permute-start | bytes 776 | tf_op jit(solution)/shard_map/while/body/eval_jaxpr/ppermute | solution.py:19
  89.0 6.4 %collective-permute-start.2 = (f32[1,64]{1,0:T(1,128)S(1)}, f32[1,64]{1,0:T(1,128)S(1)}, u32[]{:S(2)}, u32[]{:S(2)}) collective-permute-start(f32[1,64]{1,0:T(1,128)S(1)} %get-tuple-element.300), channel_id=1, source_target_pairs={{28,0},{0,4},{4,8},{8,12},{12,16},{16,20},{20,24},{24,28},{29,1},{... | collective-permute-start | bytes 776 | tf_op jit(solution)/shard_map/while/body/eval_jaxpr/ppermute | solution.py:19
  96.9 4.0 %copy-start.1 = (bf16[4096,576]{0,1:T(8,128)(2,1)S(1)}, bf16[4096,576]{0,1:T(8,128)(2,1)}, u32[]{:S(2)}) copy-start(bf16[4096,576]{0,1:T(8,128)(2,1)} %get-tuple-element.336) | copy-start | bytes 14155780 | tf_op jit(solution)/shard_map/while
  103.2 7.0 %collective-permute-start.3 = (f32[1,64,512]{2,1,0:T(8,128)S(1)}, f32[1,64,512]{2,1,0:T(8,128)}, u32[]{:S(2)}, u32[]{:S(2)}) collective-permute-start(f32[1,64,512]{2,1,0:T(8,128)S(1)} %fusion.112), channel_id=1, source_target_pairs={{28,0},{0,4},{4,8},{8,12},{12,16},{16,20},{20,24},{24,28},{29,1},{... | collective-permute-start | bytes 393224 | tf_op jit(solution)/shard_map/while/body/eval_jaxpr/ppermute | solution.py:19
  103.3 6.9 %collective-permute-start = (bf16[1,36864]{1,0:T(2,128)(2,1)S(1)}, bf16[1,36864]{1,0:T(2,128)(2,1)S(1)}, u32[]{:S(2)}, u32[]{:S(2)}) collective-permute-start(bf16[1,36864]{1,0:T(2,128)(2,1)S(1)} %copy.27), channel_id=1, source_target_pairs={{28,0},{0,4},{4,8},{8,12},{12,16},{16,20},{20,24},{24,28},{29,1},{... | collective-permute-start | bytes 221192 | tf_op jit(solution)/shard_map/while/body/eval_jaxpr/ppermute | solution.py:19
  103.4 6.8 %collective-permute-start.1 = (f32[1,64]{1,0:T(1,128)S(1)}, f32[1,64]{1,0:T(1,128)S(1)}, u32[]{:S(2)}, u32[]{:S(2)}) collective-permute-start(f32[1,64]{1,0:T(1,128)S(1)} %get-tuple-element.299), channel_id=1, source_target_pairs={{28,0},{0,4},{4,8},{8,12},{12,16},{16,20},{20,24},{24,28},{29,1},{... | collective-permute-start | bytes 776 | tf_op jit(solution)/shard_map/while/body/eval_jaxpr/ppermute | solution.py:19
  103.8 6.4 %collective-permute-start.2 = (f32[1,64]{1,0:T(1,128)S(1)}, f32[1,64]{1,0:T(1,128)S(1)}, u32[]{:S(2)}, u32[]{:S(2)}) collective-permute-start(f32[1,64]{1,0:T(1,128)S(1)} %get-tuple-element.300), channel_id=1, source_target_pairs={{28,0},{0,4},{4,8},{8,12},{12,16},{16,20},{20,24},{24,28},{29,1},{... | collective-permute-start | bytes 776 | tf_op jit(solution)/shard_map/while/body/eval_jaxpr/ppermute | solution.py:19
  111.7 4.0 %copy-start.1 = (bf16[4096,576]{0,1:T(8,128)(2,1)S(1)}, bf16[4096,576]{0,1:T(8,128)(2,1)}, u32[]{:S(2)}) copy-start(bf16[4096,576]{0,1:T(8,128)(2,1)} %get-tuple-element.336) | copy-start | bytes 14155780 | tf_op jit(solution)/shard_map/while
  118.0 7.0 %collective-permute-start.3 = (f32[1,64,512]{2,1,0:T(8,128)S(1)}, f32[1,64,512]{2,1,0:T(8,128)}, u32[]{:S(2)}, u32[]{:S(2)}) collective-permute-start(f32[1,64,512]{2,1,0:T(8,128)S(1)} %fusion.112), channel_id=1, source_target_pairs={{28,0},{0,4},{4,8},{8,12},{12,16},{16,20},{20,24},{24,28},{29,1},{... | collective-permute-start | bytes 393224 | tf_op jit(solution)/shard_map/while/body/eval_jaxpr/ppermute | solution.py:19
  118.1 6.9 %collective-permute-start = (bf16[1,36864]{1,0:T(2,128)(2,1)S(1)}, bf16[1,36864]{1,0:T(2,128)(2,1)S(1)}, u32[]{:S(2)}, u32[]{:S(2)}) collective-permute-start(bf16[1,36864]{1,0:T(2,128)(2,1)S(1)} %copy.27), channel_id=1, source_target_pairs={{28,0},{0,4},{4,8},{8,12},{12,16},{16,20},{20,24},{24,28},{29,1},{... | collective-permute-start | bytes 221192 | tf_op jit(solution)/shard_map/while/body/eval_jaxpr/ppermute | solution.py:19
  118.2 6.8 %collective-permute-start.1 = (f32[1,64]{1,0:T(1,128)S(1)}, f32[1,64]{1,0:T(1,128)S(1)}, u32[]{:S(2)}, u32[]{:S(2)}) collective-permute-start(f32[1,64]{1,0:T(1,128)S(1)} %get-tuple-element.299), channel_id=1, source_target_pairs={{28,0},{0,4},{4,8},{8,12},{12,16},{16,20},{20,24},{24,28},{29,1},{... | collective-permute-start | bytes 776 | tf_op jit(solution)/shard_map/while/body/eval_jaxpr/ppermute | solution.py:19
  118.6 6.4 %collective-permute-start.2 = (f32[1,64]{1,0:T(1,128)S(1)}, f32[1,64]{1,0:T(1,128)S(1)}, u32[]{:S(2)}, u32[]{:S(2)}) collective-permute-start(f32[1,64]{1,0:T(1,128)S(1)} %get-tuple-element.300), channel_id=1, source_target_pairs={{28,0},{0,4},{4,8},{8,12},{12,16},{16,20},{20,24},{24,28},{29,1},{... | collective-permute-start | bytes 776 | tf_op jit(solution)/shard_map/while/body/eval_jaxpr/ppermute | solution.py:19
  126.5 4.0 %copy-start.1 = (bf16[4096,576]{0,1:T(8,128)(2,1)S(1)}, bf16[4096,576]{0,1:T(8,128)(2,1)}, u32[]{:S(2)}) copy-start(bf16[4096,576]{0,1:T(8,128)(2,1)} %get-tuple-element.336) | copy-start | bytes 14155780 | tf_op jit(solution)/shard_map/while
  132.8 7.0 %collective-permute-start.3 = (f32[1,64,512]{2,1,0:T(8,128)S(1)}, f32[1,64,512]{2,1,0:T(8,128)}, u32[]{:S(2)}, u32[]{:S(2)}) collective-permute-start(f32[1,64,512]{2,1,0:T(8,128)S(1)} %fusion.112), channel_id=1, source_target_pairs={{28,0},{0,4},{4,8},{8,12},{12,16},{16,20},{20,24},{24,28},{29,1},{... | collective-permute-start | bytes 393224 | tf_op jit(solution)/shard_map/while/body/eval_jaxpr/ppermute | solution.py:19
  132.9 6.9 %collective-permute-start = (bf16[1,36864]{1,0:T(2,128)(2,1)S(1)}, bf16[1,36864]{1,0:T(2,128)(2,1)S(1)}, u32[]{:S(2)}, u32[]{:S(2)}) collective-permute-start(bf16[1,36864]{1,0:T(2,128)(2,1)S(1)} %copy.27), channel_id=1, source_target_pairs={{28,0},{0,4},{4,8},{8,12},{12,16},{16,20},{20,24},{24,28},{29,1},{... | collective-permute-start | bytes 221192 | tf_op jit(solution)/shard_map/while/body/eval_jaxpr/ppermute | solution.py:19
  133.0 6.8 %collective-permute-start.1 = (f32[1,64]{1,0:T(1,128)S(1)}, f32[1,64]{1,0:T(1,128)S(1)}, u32[]{:S(2)}, u32[]{:S(2)}) collective-permute-start(f32[1,64]{1,0:T(1,128)S(1)} %get-tuple-element.299), channel_id=1, source_target_pairs={{28,0},{0,4},{4,8},{8,12},{12,16},{16,20},{20,24},{24,28},{29,1},{... | collective-permute-start | bytes 776 | tf_op jit(solution)/shard_map/while/body/eval_jaxpr/ppermute | solution.py:19
  133.4 6.4 %collective-permute-start.2 = (f32[1,64]{1,0:T(1,128)S(1)}, f32[1,64]{1,0:T(1,128)S(1)}, u32[]{:S(2)}, u32[]{:S(2)}) collective-permute-start(f32[1,64]{1,0:T(1,128)S(1)} %get-tuple-element.300), channel_id=1, source_target_pairs={{28,0},{0,4},{4,8},{8,12},{12,16},{16,20},{20,24},{24,28},{29,1},{... | collective-permute-start | bytes 776 | tf_op jit(solution)/shard_map/while/body/eval_jaxpr/ppermute | solution.py:19
  139.8 12.3 %copy-start.4 = (s32[8]{0:T(128)S(1)}, s32[8]{0:T(128)}, u32[]{:S(2)}) copy-start(s32[8]{0:T(128)} %param.18) | copy-start | bytes 100
  139.9 17.5 %copy-start.5 = (bf16[4,1024,16]{1,2,0:T(8,128)(2,1)S(1)}, bf16[4,1024,16]{1,2,0:T(8,128)(2,1)}, u32[]{:S(2)}) copy-start(bf16[4,1024,16]{1,2,0:T(8,128)(2,1)} %param.28) | copy-start | bytes 393220
  139.9 17.8 %copy-start.2 = (bf16[4,16,7168]{2,1,0:T(8,128)(2,1)S(1)}, bf16[4,16,7168]{2,1,0:T(8,128)(2,1)}, u32[]{:S(2)}) copy-start(bf16[4,16,7168]{2,1,0:T(8,128)(2,1)} %param.29) | copy-start | bytes 2752516
  148.6 8.6 %all-to-all-start = ((bf16[8,1,8,512]{3,2,1,0:T(8,128)(2,1)}), bf16[8,1,8,512]{3,2,1,0:T(8,128)(2,1)S(1)}, u32[]{:S(2)}, u32[]{:S(2)}) async-start(bf16[8,1,8,512]{3,2,1,0:T(8,128)(2,1)} %constant_dynamic-update-slice_fusion), calls=%async_computation | async-start | bytes 131072 | tf_op jit(solution)/shard_map/all_to_all | solution.py:83
  152.1 66.0 %all-reduce.3.cloned.1.call-start = ((), (), s32[]{:S(2)}) async-start(), calls=%async_computation.1 | async-start | bytes 229376
  158.7 7.9 %copy-start.6 = (u32[32]{0:T(128)S(1)}, u32[32]{0:T(128)}, u32[]{:S(2)}) copy-start(u32[32]{0:T(128)} %constant.119) | copy-start | bytes 388
Sparse Core Ops, SparseCore 0:
  166.7 51.3 all-reduce.2
